TPU v7x, 32 devices: a whole 2x2x4 slice. The times are simulated.
32 devices in a mesh: tile: 8 (over z, x), beam: 4 (over y, core).
Axes of the slice: x: 2, y: 2, z: 4, core: 2. Of those that a mesh axis runs over, the one named last changes fastest.
Arguments:
- smatrix: bfloat16 [2, 2048, 512, 512], P(None, ('beam', 'tile')), may hold values from -6 to 6
- offset_y: int32 [128], replicated, may hold values from 0 to 511, as said below
- offset_x: int32 [128], replicated, may hold values from 0 to 511
- beam_qx: int32 [2048], P('beam'), may hold values from -64 to 63
- beam_qy: int32 [2048], P('beam'), may hold values from -64 to 63
- beam_amp: float32 [2048], P('beam'), may hold values from 0.5 to 2
- beam_phase: float32 [2048], P('beam'), may hold values from -3.140625 to 3.140625
Outputs:
- intensity: float32 [128, 128, 128], P(('tile', 'beam'))
Inputs may be any that keep to these rules, and one draw needn't show every extreme that they name: `offset_y`: the window of position p starts in field rows 64 * (p // 16) to 64 * (p // 16) + 63.
All inputs are finite; a program needn't handle non-finite values.
Results may differ from a plain program's by a relative error of at most 0.017.
Values may be sent and summed in bfloat16 or wider, within the bound.
No kernel may reach another device: no remote copies, remote signals or barrier semaphores. Data moves between devices by JAX's collectives and lax.ppermute only.
A program may use at most 256 MiB of HBM per device.

v0:
```python
import math

import jax
import jax.numpy as jnp
from jax import lax
from jax.sharding import PartitionSpec as P

BEAMS = 2048
CROP = 128
POS_DEV = 16


two_pi = 2.0 * math.pi


def passed_along(value, axis, steps):
    count = lax.axis_size(axis)
    pairs = [(source, (source + steps) % count) for source in range(count)]
    return lax.ppermute(value, axis, pairs)


def cut_window(piece, begin):
    return lax.dynamic_slice_in_dim(piece, begin, CROP, 1)


def cut_columns(piece, begin):
    return lax.dynamic_slice_in_dim(piece, begin, CROP, 2)


def transform(exit_wave):
    places = jnp.arange(CROP, dtype=jnp.int32)
    ticks = places[:, None] * places[None, :] % CROP
    angle = two_pi * ticks.astype(jnp.float32) / CROP
    norm_factor = 1.0 / math.sqrt(CROP)
    table_re = jnp.cos(angle) * norm_factor
    table_im = -jnp.sin(angle) * norm_factor
    highest = lax.Precision.HIGHEST
    right_table = jnp.concatenate(
        [
            jnp.concatenate([table_re, table_im], axis=1),
            jnp.concatenate([-table_im, table_re], axis=1),
        ],
        axis=0,
    )
    left_table = jnp.concatenate(
        [
            jnp.concatenate([table_re, -table_im], axis=1),
            jnp.concatenate([table_im, table_re], axis=1),
        ],
        axis=0,
    )
    count = exit_wave.shape[0]
    joined = jnp.concatenate([exit_wave[:, 0], exit_wave[:, 1]], axis=2)
    halves = jnp.einsum("pij,jk->pik", joined, right_table, precision=highest)
    halves = (
        halves.reshape(count, CROP, 2, CROP).transpose(0, 2, 1, 3).reshape(count, 2 * CROP, CROP)
    )
    full = jnp.einsum("ui,pik->puk", left_table, halves, precision=highest)
    full_re = full[:, :CROP]
    full_im = full[:, CROP:]
    return full_re * full_re + full_im * full_im


def local(smatrix, offset_y, offset_x, beam_qx, beam_qy, beam_amp, beam_phase):
    tiles = lax.axis_size("tile")
    own_tile = lax.axis_index("tile")
    own_group = lax.axis_index("beam")
    strips = lax.all_to_all(smatrix, "tile", split_axis=2, concat_axis=1, tiled=True)
    planes, group_beams, strip, field = strips.shape
    stacked = strips.reshape(planes * group_beams, strip * field)
    reach = CROP // strip
    scale = beam_amp * (1.0 / math.sqrt(BEAMS))

    def owner_block(distance):
        owner = (own_tile - distance) % tiles
        start = owner * POS_DEV
        first_y = lax.dynamic_slice_in_dim(offset_y, start, POS_DEV)
        first_x = lax.dynamic_slice_in_dim(offset_x, start, POS_DEV)
        turns = (
            (first_x + CROP // 2)[:, None] * beam_qx[None, :]
            + (first_y + CROP // 2)[:, None] * beam_qy[None, :]
        ) % field
        angle = beam_phase[None, :] - two_pi * turns.astype(jnp.float32) / field
        w_real = (scale[None, :] * jnp.cos(angle)).astype(jnp.bfloat16)
        w_imag = (scale[None, :] * jnp.sin(angle)).astype(jnp.bfloat16)
        real_row = jnp.concatenate([w_real, -w_imag], axis=1)
        imag_row = jnp.concatenate([w_imag, w_real], axis=1)
        mixing = jnp.stack([real_row, imag_row], axis=1).reshape(2 * POS_DEV, 2 * group_beams)
        waves = jnp.dot(mixing, stacked, preferred_element_type=jnp.float32).astype(jnp.bfloat16)
        waves = waves.reshape(POS_DEV, 2, strip, field)
        extended = jnp.concatenate([waves, waves[:, :, :, :CROP]], axis=3)
        return jax.vmap(cut_columns)(extended, first_x % field)

    blocks = jnp.stack([owner_block(distance) for distance in range(reach + 1)])
    reduced = lax.psum_scatter(
        blocks.astype(jnp.float32).astype(jnp.bfloat16), "beam", scatter_dimension=1, tiled=True
    ).astype(jnp.float32)
    pieces = [reduced[0]]
    for distance in range(1, reach + 1):
        pieces.append(passed_along(reduced[distance], "tile", -distance))
    gathered = jnp.concatenate(pieces, axis=2)
    share = POS_DEV // lax.axis_size("beam")
    first_rows = (
        lax.dynamic_slice_in_dim(offset_y, own_tile * POS_DEV + own_group * share, share) % strip
    )
    exit_wave = jax.vmap(cut_window)(gathered, first_rows)
    return transform(exit_wave)


def solution(mesh):
    return jax.shard_map(
        local,
        mesh=mesh,
        in_specs=(
            P(None, ("beam", "tile"), None, None),
            P(),
            P(),
            P("beam"),
            P("beam"),
            P("beam"),
            P("beam"),
        ),
        out_specs=P(("tile", "beam"), None, None),
        check_vma=False,
    )
```

profile of v0, /device:TPU:0, one launch (start us, length us, event | category | flops | bytes accessed | tf_op | source)
XLA Modules:
  0.0 1897.7 jit_solution(9483765150385757579)
XLA Ops:
  6.5 59.4 %copy.50 = bf16[2,64,512,512]{3,1,0,2:T(8,128)(2,1)} copy(bf16[2,64,512,512]{3,2,1,0:T(8,128)(2,1)} %param.7) | data formatting | bytes 134217728 | tf_op args[0]
  66.0 10.0 all-to-all-start
  76.0 0.2 reduce-scatter.2.cloned.1.call-start
  76.5 0.5 fusion.60
  76.9 0.5 multiply_convert_fusion.4
  77.9 0.7 fusion.57
  78.5 1440.7 %all-to-all-done = bf16[2,64,512,512]{3,1,0,2:T(8,128)(2,1)} async-done(((bf16[2,64,512,512]{3,1,0,2:T(8,128)(2,1)}), bf16[2,64,512,512]{3,1,0,2:T(8,128)(2,1)}, u32[]{:S(2)}, u32[]{:S(2)}) %all-to-all-start) | async-done | bytes 67108896 | tf_op jit(solution)/shard_map/all_to_all | solution.py:68
  1519.3 59.8 %copy.51 = bf16[2,64,8,64,512]{4,3,1,2,0:T(8,128)(2,1)} copy(bf16[2,64,8,64,512]{4,1,0,3,2:T(8,128)(2,1)} %bitcast.2) | data formatting | bytes 134217728 | tf_op jit(solution)/shard_map/all_to_all | solution.py:68
  1579.1 59.2 %copy.68 = bf16[128,8,64,512]{3,1,2,0:T(8,128)(2,1)} copy(bf16[128,8,64,512]{3,2,1,0:T(8,128)(2,1)} %bitcast.33) | data formatting | bytes 134217728
  1638.3 23.6 %convolution_convert_fusion.2 = bf16[32,32768]{1,0:T(8,128)(2,1)S(1)} fusion(bf16[32,1024]{1,0:T(8,128)(2,1)S(1)} %reshape.38, bf16[1024,32768]{1,0:T(8,128)(2,1)} %bitcast.34), kind=kOutput, calls=%fused_computation.6 | convolution fusion | flops 2148532224 | bytes 69271552 | tf_op jit(solution)/shard_map/dot_general | solution.py:89
  1661.9 2.0 copy.69
  1663.9 10.9 copy.53
  1674.9 1.9 slice.65
  1676.8 18.0 pad_maximum_fusion
  1694.8 23.8 %convolution_convert_fusion.1 = bf16[32,32768]{1,0:T(8,128)(2,1)S(1)} fusion(bf16[32,1024]{1,0:T(8,128)(2,1)S(1)} %reshape.41, bf16[1024,32768]{1,0:T(8,128)(2,1)} %bitcast.34), kind=kOutput, calls=%fused_computation.5 | convolution fusion | flops 2148532224 | bytes 69271552 | tf_op jit(solution)/shard_map/dot_general | solution.py:89
  1718.6 2.0 copy.70
  1720.7 10.9 copy.56
  1731.6 1.9 slice.66
  1733.5 18.0 pad_maximum_fusion.1
  1751.6 23.6 %convolution_convert_fusion = bf16[32,32768]{1,0:T(8,128)(2,1)S(1)} fusion(bf16[32,1024]{1,0:T(8,128)(2,1)S(1)} %reshape.43, bf16[1024,32768]{1,0:T(8,128)(2,1)} %bitcast.34), kind=kOutput, calls=%fused_computation.4 | convolution fusion | flops 2148532224 | bytes 69271552 | tf_op jit(solution)/shard_map/dot_general | solution.py:89
  1775.2 2.1 copy.71
  1777.2 10.9 copy.59
  1788.2 1.9 slice.67
  1790.2 18.4 pad_maximum_fusion.2
  1808.6 6.7 gather_fusion
  1815.3 6.7 gather_fusion.1
  1822.1 6.8 gather_fusion.2
  1828.9 7.4 pad_maximum_fusion.3
  1836.3 5.0 copy.60
  1841.3 27.1 %reduce-scatter.2.cloned.1.call-done = bf16[3,4,2,64,128]{4,3,2,0,1:T(8,128)(2,1)} async-done(((bf16[3,16,2,64,128]{4,3,2,0,1:T(8,128)(2,1)}), bf16[3,4,2,64,128]{4,3,2,0,1:T(8,128)(2,1)}) %reduce-scatter.2.cloned.1.call-update) | async-done | bytes 393232 | tf_op jit(solution)/shard_map/reduce_scatter | solution.py:95
  1868.5 1.4 copy_convert_fusion
  1869.9 0.3 slice_bitcast_fusion.2
  1870.2 4.3 collective-permute-start
  1874.5 0.7 collective-permute-start.1
  1875.1 0.1 fusion.54
  1875.2 0.3 fusion.33
  1875.5 0.3 negate_multiply_fusion
  1875.8 5.4 collective-permute-done
  1881.2 4.3 collective-permute-done.1
  1885.5 0.3 pad_maximum_fusion.4
  1885.8 1.3 gather_fusion.3
  1887.1 0.4 fusion.63
  1887.5 0.6 fusion
  1888.1 0.3 reshape.45
  1888.4 0.4 copy.64
  1888.8 0.4 reshape.46
  1889.2 0.6 convolution_bitcast_fusion
  1889.9 0.8 copy.65
  (36 shorter events, 0.5 us)
Async XLA Ops:
  66.0 10.3 copy-start.3
  66.0 10.4 copy-start.7
  66.0 10.4 copy-start.9
  66.0 10.4 copy-start.4
  66.0 10.4 copy-start.5
  66.0 10.4 copy-start.6
  66.0 1453.2 %all-to-all-start = ((bf16[2,64,512,512]{3,1,0,2:T(8,128)(2,1)}), bf16[2,64,512,512]{3,1,0,2:T(8,128)(2,1)}, u32[]{:S(2)}, u32[]{:S(2)}) async-start(bf16[2,64,512,512]{3,1,0,2:T(8,128)(2,1)} %copy.50), calls=%async_computation | async-start | bytes 134217728 | tf_op jit(solution)/shard_map/all_to_all | solution.py:68
  76.0 1792.5 %reduce-scatter.2.cloned.1.call-start = ((), (), s32[]{:S(2)}) async-start(), calls=%async_computation.2 | async-start | bytes 1966080 | tf_op jit(solution)/shard_map/reduce_scatter | solution.py:95
  1790.1 18.4 copy-start.2
  1790.1 25.2 %copy-start.1 = (s32[16]{0:T(128)S(1)}, s32[16]{0:T(128)}, u32[]{:S(2)}) copy-start(s32[16]{0:T(128)} %get-tuple-element.30) | copy-start | bytes 196
  1790.1 31.9 %copy-start = (s32[16]{0:T(128)S(1)}, s32[16]{0:T(128)}, u32[]{:S(2)}) copy-start(s32[16]{0:T(128)} %get-tuple-element.31) | copy-start | bytes 196
  1836.3 38.9 %copy-start.8 = (s32[128]{0:T(128)S(1)}, s32[128]{0:T(128)}, u32[]{:S(2)}) copy-start(s32[128]{0:T(128)} %param.8) | copy-start | bytes 1540
  1870.2 11.0 collective-permute-start
  1874.5 11.0 collective-permute-start.1
Sparse Core Ops, SparseCore 0:
  1841.5 26.9 reduce-scatter.1
where the time goes:
time: 1900 us
  waiting for transfers between devices  1480 us (78%)
  local copies, waits for them, and re-layouts  253 us (13%)
  matrix products  72.2 us (4%)
  other arithmetic  66 us (3%)
    all_to_all x1, waiting for transfers between devices, local(): lax.all_to_all(smatrix, 'tile', split_axis=2, concat_axis=1, tiled=True)  1440 us
    unnamed x25, local copies, waits for them, and re-layouts  125 us
    dot_general x3, matrix products, owner_block(): jnp.dot(mixing, stacked, preferred_element_type=jnp.float32)  71 us
    all_to_all x1, local copies, waits for them, and re-layouts, local(): lax.all_to_all(smatrix, 'tile', split_axis=2, concat_axis=1, tiled=True)  59.8 us
    concatenate x3, other arithmetic, owner_block(): extended = jnp.concatenate([waves, waves[:, :, :, :CROP]], axis=3)  54.5 us
  transfers between devices with their start and end apart: 4, of which 4 were waited for; matrix products, arithmetic and copies ran while one was open for 0% of the time, Pallas kernels for 0%

commit v1 on v0

v1 whole, which is shorter than its diff:
```python
import functools
import math

import jax
import jax.numpy as jnp
from jax import lax
from jax.experimental import pallas as pl
from jax.experimental.pallas import tpu as pltpu
from jax.sharding import PartitionSpec as P

BEAMS = 2048
CROP = 128
POS_DEV = 16
ROWS = 8
CHUNKS = 4

two_pi = 2.0 * math.pi


def exchanged(value, axis, bit):
    count = lax.axis_size(axis)
    return lax.ppermute(value, axis, [(i, i ^ bit) for i in range(count)])


def waves_kernel(
    tiles, beams, first_step, tile_ref, s_ref, w_ref, block_ref, low_ref, keep_ref, send_ref, rows_ref
):
    planes, group, turns, _, field = s_ref.shape
    depth = planes * group
    strip = field // tiles
    reach = CROP // strip
    per_owner = 2 * POS_DEV
    base_row = (pl.program_id(0) + first_step) * ROWS
    strip_at = base_row // strip
    row_in_strip = base_row % strip
    own_tile = tile_ref[0]
    half = per_owner // 2
    groups = field // CROP

    for k in range(turns):
        for c in range(groups):
            piece = s_ref[:, :, k, :, c * CROP : (c + 1) * CROP].astype(jnp.float32)
            rows_ref[k, c] = piece.reshape(depth * ROWS, CROP)

    def one_row(r, carry):
        late = None
        first = None
        for k in range(turns):
            start = pl.multiple_of((reach * k + strip_at) * per_owner, per_owner)
            count = (reach + 1) * per_owner
            values = [
                rows_ref[k, c, pl.ds(r, depth, stride=ROWS), :].astype(jnp.bfloat16)
                for c in range(groups)
            ]
            values = jnp.concatenate(values, axis=1)
            out = jnp.dot(
                w_ref[pl.ds(start, count), :], values, preferred_element_type=jnp.float32
            )
            block = block_ref[pl.ds(start, count), :]
            folded = out[:, (groups - 1) * CROP :]
            for c in range(groups - 1):
                folded = jnp.where(block == c, out[:, c * CROP : (c + 1) * CROP], folded)
            low = low_ref[pl.ds(start, per_owner), :]
            yield_k = (folded, low)
            if k == 0:
                first = yield_k
            else:
                store(r, k, late, yield_k)
            late = folded
        store(r, turns, late, first)
        return carry

    def store(r, k, before, here):
        folded, low = here
        for e in range(reach):
            owner = (reach * (k - 1) + strip_at + e) % tiles
            part = folded[e * per_owner : (e + 1) * per_owner]
            if e == 0:
                began = before[reach * per_owner :]
                part = jnp.where(low <= row_in_strip + r, began, part)
            part = part.astype(jnp.bfloat16)
            place = owner ^ own_tile
            keep_ref[r, place] = part[:half]
            send_ref[r, place] = part[half:]

    for r in range(ROWS):
        one_row(r, 0)


def partial_waves(chunk, smatrix, own_tile, weights, block, low):
    planes, group, field, _ = smatrix.shape
    tiles = lax.axis_size("tile")
    beams = lax.axis_size("beam")
    rows = CROP // CHUNKS
    steps = rows // ROWS
    turns = field // CROP
    viewed = smatrix.reshape(planes, group, turns, CROP, field)
    half = POS_DEV
    shape = jax.ShapeDtypeStruct((rows, tiles, half, CROP), jnp.bfloat16)
    out_spec = pl.BlockSpec((ROWS, tiles, half, CROP), lambda i, t: (i, 0, 0, 0))
    whole = pl.BlockSpec(memory_space=pltpu.VMEM)
    first_step = chunk * steps
    flops = 2 * 3 * 2 * POS_DEV * planes * group * field * field // CHUNKS
    return pl.pallas_call(
        functools.partial(waves_kernel, tiles, beams, first_step),
        out_shape=(shape, shape),
        grid_spec=pltpu.PrefetchScalarGridSpec(
            num_scalar_prefetch=1,
            grid=(steps,),
            in_specs=[
                pl.BlockSpec(
                    (planes, group, turns, ROWS, field), lambda i, t: (0, 0, 0, i + first_step, 0)
                ),
                whole,
                whole,
                whole,
            ],
            out_specs=(out_spec, out_spec),
            scratch_shapes=[
                pltpu.VMEM((turns, field // CROP, planes * group * ROWS, CROP), jnp.float32)
            ],
        ),
        compiler_params=pltpu.CompilerParams(vmem_limit_bytes=48 * 1024 * 1024),
        cost_estimate=pl.CostEstimate(
            flops=flops,
            bytes_accessed=smatrix.size * 2 // CHUNKS,
            transcendentals=0,
        ),
        name=f"waves_{chunk}",
    )(own_tile, viewed, weights, block, low)


def intensity_kernel(share, wave_ref, right_ref, left_ref, out_ref, rows_ref):
    rows_ref[...] = wave_ref[...].reshape(CROP * 2 * share, CROP)
    for q in range(share):
        real = rows_ref[pl.ds(2 * q, CROP, stride=2 * share), :]
        imag = rows_ref[pl.ds(2 * q + 1, CROP, stride=2 * share), :]
        joined = jnp.concatenate([real, imag], axis=1)
        halves = jnp.dot(
            joined, right_ref[...], precision=lax.Precision.HIGHEST,
            preferred_element_type=jnp.float32,
        )
        halves = jnp.concatenate([halves[:, :CROP], halves[:, CROP:]], axis=0)
        full = jnp.dot(
            left_ref[...], halves, precision=lax.Precision.HIGHEST,
            preferred_element_type=jnp.float32,
        )
        full_re, full_im = full[:CROP], full[CROP:]
        out_ref[q] = full_re * full_re + full_im * full_im


def intensities(waves):
    share = waves.shape[1] // 2
    places = jnp.arange(CROP, dtype=jnp.int32)
    ticks = places[:, None] * places[None, :] % CROP
    angle = two_pi * ticks.astype(jnp.float32) / CROP
    norm_factor = 1.0 / math.sqrt(CROP)
    table_re = jnp.cos(angle) * norm_factor
    table_im = -jnp.sin(angle) * norm_factor
    right = jnp.concatenate(
        [
            jnp.concatenate([table_re, table_im], axis=1),
            jnp.concatenate([-table_im, table_re], axis=1),
        ],
        axis=0,
    )
    left = jnp.concatenate(
        [
            jnp.concatenate([table_re, -table_im], axis=1),
            jnp.concatenate([table_im, table_re], axis=1),
        ],
        axis=0,
    )
    return pl.pallas_call(
        functools.partial(intensity_kernel, share),
        out_shape=jax.ShapeDtypeStruct((share, CROP, CROP), jnp.float32),
        in_specs=[pl.BlockSpec(memory_space=pltpu.VMEM)] * 3,
        out_specs=pl.BlockSpec(memory_space=pltpu.VMEM),
        scratch_shapes=[pltpu.VMEM((CROP * 2 * share, CROP), jnp.float32)],
        name="intensity",
    )(waves, right, left)


def local(smatrix, offset_y, offset_x, beam_qx, beam_qy, beam_amp, beam_phase):
    tiles = lax.axis_size("tile")
    beams = lax.axis_size("beam")
    own_tile = lax.axis_index("tile")
    own_group = lax.axis_index("beam")
    planes, group, field, _ = smatrix.shape
    strip = field // tiles
    reach = CROP // strip
    share = POS_DEV // beams

    places = jnp.arange(beams, dtype=jnp.int32)
    order = (places % (beams // 2) * 2 + places // (beams // 2)) ^ own_group
    first_y = offset_y.reshape(tiles, beams, share)[:, order].reshape(tiles * POS_DEV)
    first_x = offset_x.reshape(tiles, beams, share)[:, order].reshape(tiles * POS_DEV)
    begin = own_tile * group
    qx = lax.dynamic_slice_in_dim(beam_qx, begin, group)
    qy = lax.dynamic_slice_in_dim(beam_qy, begin, group)
    amp = lax.dynamic_slice_in_dim(beam_amp, begin, group)
    phase = lax.dynamic_slice_in_dim(beam_phase, begin, group)
    scale = amp * (1.0 / math.sqrt(BEAMS))
    turns = (
        (first_x + CROP // 2)[:, None] * qx[None, :]
        + (first_y + CROP // 2)[:, None] * qy[None, :]
    ) % field
    angle = phase[None, :] - two_pi * turns.astype(jnp.float32) / field
    w_real = (scale[None, :] * jnp.cos(angle)).astype(jnp.bfloat16)
    w_imag = (scale[None, :] * jnp.sin(angle)).astype(jnp.bfloat16)
    real_row = jnp.concatenate([w_real, -w_imag], axis=1)
    imag_row = jnp.concatenate([w_imag, w_real], axis=1)
    weights = jnp.stack([real_row, imag_row], axis=1).reshape(tiles * 2 * POS_DEV, planes * group)
    lanes = jnp.arange(CROP, dtype=jnp.int32)
    wraps = (first_x % field // CROP)[:, None] + (lanes[None, :] < (first_x % CROP)[:, None])
    block = jnp.repeat(wraps % (field // CROP), 2, axis=0).astype(jnp.int32)
    low = jnp.broadcast_to(jnp.repeat(first_y % strip, 2)[:, None], block.shape).astype(jnp.int32)

    def wrapped(table):
        return jnp.concatenate([table[-reach * 2 * POS_DEV :], table], axis=0)

    weights, block, low = wrapped(weights), wrapped(block), wrapped(low)
    own = own_tile.reshape(1).astype(jnp.int32)

    tile_bits = [1 << b for b in range(tiles.bit_length() - 1)]
    beam_bits = [1 << b for b in range(beams.bit_length() - 1)]
    plain = [("beam", b) for b in beam_bits[:0:-1]]
    pieces = []
    for chunk in range(CHUNKS):
        keep, send = partial_waves(chunk, smatrix, own, weights, block, low)
        pieces.append(reduce_chunk(keep, send, chunk, tile_bits, beam_bits, share))
    waves = jnp.concatenate(pieces, axis=0)
    return intensities(waves)


def reduce_chunk(keep, send, chunk, tile_bits, beam_bits, share):
    rows = keep.shape[0]
    arrived = exchanged(send, "beam", 1)
    names = [("tile", b) for b in reversed(tile_bits)]
    names += [("beam", b) for b in reversed(beam_bits[1:])]
    shape = (rows,) + (2,) * len(names) + (2 * share, CROP)
    terms = [keep.reshape(shape), arrived.reshape(shape)]
    first_tile = [("tile", tile_bits[0])]
    rest_tile = [("tile", b) for b in tile_bits[1:]]
    rest_beam = [("beam", b) for b in beam_bits[1:]]
    plan = first_tile + rest_beam if chunk % 2 == 0 else rest_beam + first_tile
    for name in plan + rest_tile:
        at = 1 + names.index(name)
        names.remove(name)
        away = [lax.index_in_dim(t, 1, at, keepdims=False).astype(jnp.float32) for t in terms]
        stay = [lax.index_in_dim(t, 0, at, keepdims=False) for t in terms]
        packed = functools.reduce(jnp.add, away).astype(jnp.bfloat16)
        terms = stay + [exchanged(packed, *name)]
    total = functools.reduce(jnp.add, [t.astype(jnp.float32) for t in terms])
    return total.reshape(rows, 2 * share, CROP)


def solution(mesh):
    return jax.shard_map(
        local,
        mesh=mesh,
        in_specs=(
            P(None, ("beam", "tile"), None, None),
            P(),
            P(),
            P("beam"),
            P("beam"),
            P("beam"),
            P("beam"),
        ),
        out_specs=P(("tile", "beam"), None, None),
        check_vma=False,
    )
```

time: 1900 us -> 130 us (0.07)
  waiting for transfers between devices: 1480 us -> 32.9 us
  local copies, waits for them, and re-layouts: 253 us -> 9.72 us
  matrix products: 72.2 us -> 0 us
  other arithmetic: 66 us -> 5.44 us
  Pallas kernels: 0 us -> 58.6 us
    all_to_all x1 -> x0, waiting for transfers between devices: 1440 us -> none  [local(): lax.all_to_all(smatrix, 'tile', split_axis=2, concat_axis=1, tiled=True)]
    unnamed x25 -> x8, local copies, waits for them, and re-layouts: 125 us -> 0.74 us
    dot_general x5 -> x0, matrix products: 72.2 us -> none  [the longest x3 71 us: owner_block(): jnp.dot(mixing, stacked, preferred_element_type=jnp.float32)]
    all_to_all x1 -> x0, local copies, waits for them, and re-layouts: 59.8 us -> none  [local(): lax.all_to_all(smatrix, 'tile', split_axis=2, concat_axis=1, tiled=True)]
    pallas_call x0 -> x5, Pallas kernels: none -> 58.6 us  [the longest x4 54.8 us: partial_waves(): pl.pallas_call(functools.partial(waves_kernel, tiles, beams, first_step),...]
    concatenate x4 -> x5, other arithmetic: 54.8 us -> 1.78 us  [the longest x1 0.85 us: intensities(): jnp.concatenate([jnp.concatenate([table_re, -table_im], axis=1), jnp.conc...]
    reshape x8 -> x6, local copies, waits for them, and re-layouts: 33.6 us -> 1.96 us  [the longest x3 0.98 us: local(): offset_y.reshape(tiles, beams, share)[:, order].reshape(tiles * POS_DEV)]
    reduce_scatter x1 -> x0, waiting for transfers between devices: 27.1 us -> none  [local(): lax.psum_scatter(blocks.astype(jnp.float32).astype(jnp.bfloat16), 'beam',...]
  transfers between devices with their start and end apart: 4 -> 20, of which waited for: 4 -> 10; matrix products, arithmetic and copies ran while one was open for 0% -> 5% of each run, Pallas kernels for 0% -> 32%
where the time goes in v1:
time: 130 us
  Pallas kernels  58.6 us (45%)
  waiting for transfers between devices  32.9 us (25%)
  starting transfers between devices  22.5 us (17%)
  local copies, waits for them, and re-layouts  9.72 us (7%)
  other arithmetic  5.44 us (4%)
    pallas_call x4, Pallas kernels, partial_waves(): pl.pallas_call(functools.partial(waves_kernel, tiles, beams, first_step),...  54.8 us
    ppermute x20, waiting for transfers between devices, exchanged(): return lax.ppermute(value, axis, [(i, i ^ bit) for i in range(count)])  32.9 us
    ppermute x20, starting transfers between devices, exchanged(): return lax.ppermute(value, axis, [(i, i ^ bit) for i in range(count)])  22.5 us
    pallas_call x1, Pallas kernels, intensities(): pl.pallas_call(functools.partial(intensity_kernel, share), out_shape=jax....  3.79 us
  transfers between devices with their start and end apart: 20, of which 10 were waited for; matrix products, arithmetic and copies ran while one was open for 5% of the time, Pallas kernels for 32%

profile of v1, /device:TPU:0, one launch (start us, length us, event | category | flops | bytes accessed | tf_op | source)
XLA Modules:
  0.0 129.8 jit_solution(4367778887443126709)
XLA Ops:
  0.0 0.8 dynamic-slice_multiply_fusion
  0.8 0.8 dynamic_slice.13
  1.5 0.8 dynamic_slice.14
  2.3 0.8 dynamic_slice.15
  3.0 0.8 reshape.339
  3.9 0.6 gather_fusion
  4.7 0.8 reshape.341
  5.6 0.6 gather_fusion.1
  8.1 13.6 %waves_0.1 = (bf16[32,8,16,128]{3,2,1,0:T(8,128)(2,1)S(1)}, bf16[32,8,16,128]{3,2,1,0:T(8,128)(2,1)S(1)}) custom-call(s32[1]{0:T(128)} %bitcast.tile_ref, bf16[2,64,4,128,512]{4,3,2,1,0:T(8,128)(2,1)} %bitcast.1.s_ref, bf16[320,128]{1,0:T(8,128)(2,1)S(1)} %pad_maximum_fusion.5.w_ref, s32[320,128]{1,0:T(8,128)S(1)} %pad_add_fusion.block_ref, ...), custom_call_target="tpu_custom_call" | custom-call | flops 1610612736 | bytes 16777216 | tf_op jit(solution)/shard_map/waves_0/pallas_call | solution.py:104
  21.7 0.6 collective-permute-start
  22.3 13.6 %waves_1.1 = (bf16[32,8,16,128]{3,2,1,0:T(8,128)(2,1)S(1)}, bf16[32,8,16,128]{3,2,1,0:T(8,128)(2,1)S(1)}) custom-call(s32[1]{0:T(128)} %bitcast.tile_ref, bf16[2,64,4,128,512]{4,3,2,1,0:T(8,128)(2,1)} %bitcast.1.s_ref, bf16[320,128]{1,0:T(8,128)(2,1)S(1)} %pad_maximum_fusion.5.w_ref, s32[320,128]{1,0:T(8,128)S(1)} %pad_add_fusion.block_ref, ...), custom_call_target="tpu_custom_call" | custom-call | flops 1610612736 | bytes 16777216 | tf_op jit(solution)/shard_map/waves_1/pallas_call | solution.py:104
  35.9 13.7 %waves_2.1 = (bf16[32,8,16,128]{3,2,1,0:T(8,128)(2,1)S(1)}, bf16[32,8,16,128]{3,2,1,0:T(8,128)(2,1)S(1)}) custom-call(s32[1]{0:T(128)} %bitcast.tile_ref, bf16[2,64,4,128,512]{4,3,2,1,0:T(8,128)(2,1)} %bitcast.1.s_ref, bf16[320,128]{1,0:T(8,128)(2,1)S(1)} %pad_maximum_fusion.5.w_ref, s32[320,128]{1,0:T(8,128)S(1)} %pad_add_fusion.block_ref, ...), custom_call_target="tpu_custom_call" | custom-call | flops 1610612736 | bytes 16777216 | tf_op jit(solution)/shard_map/waves_2/pallas_call | solution.py:104
  49.6 0.5 collective-permute-start.10
  50.2 13.9 %waves_3.1 = (bf16[32,8,16,128]{3,2,1,0:T(8,128)(2,1)S(1)}, bf16[32,8,16,128]{3,2,1,0:T(8,128)(2,1)S(1)}) custom-call(s32[1]{0:T(128)} %bitcast.tile_ref, bf16[2,64,4,128,512]{4,3,2,1,0:T(8,128)(2,1)} %bitcast.1.s_ref, bf16[320,128]{1,0:T(8,128)(2,1)S(1)} %pad_maximum_fusion.5.w_ref, s32[320,128]{1,0:T(8,128)S(1)} %pad_add_fusion.block_ref, ...), custom_call_target="tpu_custom_call" | custom-call | flops 1610612736 | bytes 16777216 | tf_op jit(solution)/shard_map/waves_3/pallas_call | solution.py:104
  64.7 0.3 fusion.37
  65.2 0.3 fusion.39
  66.0 0.3 fusion.43
  66.3 0.9 fusion.5
  67.6 3.0 %collective-permute-start.1 = (bf16[32,2,2,2,8,128]{5,4,0,1,2,3:T(8,128)(2,1)S(1)}, bf16[32,2,2,2,8,128]{5,4,0,1,2,3:T(8,128)(2,1)S(1)}, u32[]{:S(2)}, u32[]{:S(2)}) collective-permute-start(bf16[32,2,2,2,8,128]{5,4,0,1,2,3:T(8,128)(2,1)S(1)} %fusion), channel_id=1, source_target_pairs={{0,4},{4,0},{8,12},{12,8},{16,20},{20,16},{24,28},{28,24},{1,5},{5... | collective-permute-start | bytes 1572872 | tf_op jit(solution)/shard_map/ppermute | solution.py:22
  70.8 0.3 fusion.40
  71.2 1.6 %collective-permute-start.6 = (bf16[32,2,2,2,8,128]{5,4,0,1,2,3:T(8,128)(2,1)S(1)}, bf16[32,2,2,2,8,128]{5,4,0,1,2,3:T(8,128)(2,1)S(1)}, u32[]{:S(2)}, u32[]{:S(2)}) collective-permute-start(bf16[32,2,2,2,8,128]{5,4,0,1,2,3:T(8,128)(2,1)S(1)} %fusion.1), channel_id=1, source_target_pairs={{0,2},{1,3},{2,0},{3,1},{4,6},{5,7},{6,4},{7,5},{8,10},{9,11},{10,... | collective-permute-start | bytes 1572872 | tf_op jit(solution)/shard_map/ppermute | solution.py:22
  72.8 0.3 fusion.42
  73.4 0.6 collective-permute-start.11
  74.2 0.3 fusion.44
  74.9 8.5 %collective-permute-done.1 = bf16[32,2,2,2,8,128]{5,4,0,1,2,3:T(8,128)(2,1)S(1)} collective-permute-done((bf16[32,2,2,2,8,128]{5,4,0,1,2,3:T(8,128)(2,1)S(1)}, bf16[32,2,2,2,8,128]{5,4,0,1,2,3:T(8,128)(2,1)S(1)}, u32[]{:S(2)}, u32[]{:S(2)}) %collective-permute-start.1) | collective-permute-done | bytes 524320 | tf_op jit(solution)/shard_map/ppermute | solution.py:22
  83.5 2.1 %collective-permute-start.2 = (bf16[32,2,2,8,128]{4,3,0,1,2:T(8,128)(2,1)S(1)}, bf16[32,2,2,8,128]{4,3,0,1,2:T(8,128)(2,1)S(1)}, u32[]{:S(2)}, u32[]{:S(2)}) collective-permute-start(bf16[32,2,2,8,128]{4,3,0,1,2:T(8,128)(2,1)S(1)} %fusion.6), channel_id=1, source_target_pairs={{0,2},{1,3},{2,0},{3,1},{4,6},{5,7},{6,4},{7,5},{8,10},{9,11},{10,... | collective-permute-start | bytes 786440 | tf_op jit(solution)/shard_map/ppermute | solution.py:22
  85.6 0.4 collective-permute-done.6
  86.2 1.1 collective-permute-start.7
  87.4 7.3 %collective-permute-done.11 = bf16[32,2,2,2,8,128]{5,4,0,1,2,3:T(8,128)(2,1)S(1)} collective-permute-done((bf16[32,2,2,2,8,128]{5,4,0,1,2,3:T(8,128)(2,1)S(1)}, bf16[32,2,2,2,8,128]{5,4,0,1,2,3:T(8,128)(2,1)S(1)}, u32[]{:S(2)}, u32[]{:S(2)}) %collective-permute-start.11) | collective-permute-done | bytes 524320 | tf_op jit(solution)/shard_map/ppermute | solution.py:22
  94.8 2.1 %collective-permute-start.12 = (bf16[32,2,2,8,128]{4,3,0,1,2:T(8,128)(2,1)S(1)}, bf16[32,2,2,8,128]{4,3,0,1,2:T(8,128)(2,1)S(1)}, u32[]{:S(2)}, u32[]{:S(2)}) collective-permute-start(bf16[32,2,2,8,128]{4,3,0,1,2:T(8,128)(2,1)S(1)} %fusion.8), channel_id=1, source_target_pairs={{0,2},{1,3},{2,0},{3,1},{4,6},{5,7},{6,4},{7,5},{8,10},{9,11},{10,... | collective-permute-start | bytes 786440 | tf_op jit(solution)/shard_map/ppermute | solution.py:22
  96.9 0.4 collective-permute-done.16
  97.4 1.2 collective-permute-start.17
  98.7 4.3 %collective-permute-done.2 = bf16[32,2,2,8,128]{4,3,0,1,2:T(8,128)(2,1)S(1)} collective-permute-done((bf16[32,2,2,8,128]{4,3,0,1,2:T(8,128)(2,1)S(1)}, bf16[32,2,2,8,128]{4,3,0,1,2:T(8,128)(2,1)S(1)}, u32[]{:S(2)}, u32[]{:S(2)}) %collective-permute-start.2) | collective-permute-done | bytes 262176 | tf_op jit(solution)/shard_map/ppermute | solution.py:22
  103.0 1.6 %collective-permute-start.3 = (bf16[32,2,8,128]{3,2,0,1:T(8,128)(2,1)S(1)}, bf16[32,2,8,128]{3,2,0,1:T(8,128)(2,1)S(1)}, u32[]{:S(2)}, u32[]{:S(2)}) collective-permute-start(bf16[32,2,8,128]{3,2,0,1:T(8,128)(2,1)S(1)} %fusion.10), channel_id=1, source_target_pairs={{0,8},{4,12},{8,0},{12,4},{16,24},{20,28},{24,16},{28,20},{1,9},{5... | collective-permute-start | bytes 393224 | tf_op jit(solution)/shard_map/ppermute | solution.py:22
  104.7 0.5 collective-permute-start.8
  105.2 2.1 %collective-permute-done.12 = bf16[32,2,2,8,128]{4,3,0,1,2:T(8,128)(2,1)S(1)} collective-permute-done((bf16[32,2,2,8,128]{4,3,0,1,2:T(8,128)(2,1)S(1)}, bf16[32,2,2,8,128]{4,3,0,1,2:T(8,128)(2,1)S(1)}, u32[]{:S(2)}, u32[]{:S(2)}) %collective-permute-start.12) | collective-permute-done | bytes 262176 | tf_op jit(solution)/shard_map/ppermute | solution.py:22
  107.4 1.6 %collective-permute-start.13 = (bf16[32,2,8,128]{3,2,0,1:T(8,128)(2,1)S(1)}, bf16[32,2,8,128]{3,2,0,1:T(8,128)(2,1)S(1)}, u32[]{:S(2)}, u32[]{:S(2)}) collective-permute-start(bf16[32,2,8,128]{3,2,0,1:T(8,128)(2,1)S(1)} %fusion.12), channel_id=1, source_target_pairs={{0,8},{4,12},{8,0},{12,4},{16,24},{20,28},{24,16},{28,20},{1,9},{5... | collective-permute-start | bytes 393224 | tf_op jit(solution)/shard_map/ppermute | solution.py:22
  109.1 0.5 collective-permute-start.18
  109.8 2.6 %collective-permute-start.4 = (bf16[32,8,128]{2,1,0:T(8,128)(2,1)S(1)}, bf16[32,8,128]{2,1,0:T(8,128)(2,1)S(1)}, u32[]{:S(2)}, u32[]{:S(2)}) collective-permute-start(bf16[32,8,128]{2,1,0:T(8,128)(2,1)S(1)} %fusion.19), channel_id=1, source_target_pairs={{0,16},{4,20},{8,24},{12,28},{16,0},{20,4},{24,8},{28,12},{1,17},{... | collective-permute-start | bytes 196616 | tf_op jit(solution)/shard_map/ppermute | solution.py:22
  112.4 0.9 collective-permute-start.9
  113.3 3.3 %collective-permute-done.13 = bf16[32,2,8,128]{3,2,0,1:T(8,128)(2,1)S(1)} collective-permute-done((bf16[32,2,8,128]{3,2,0,1:T(8,128)(2,1)S(1)}, bf16[32,2,8,128]{3,2,0,1:T(8,128)(2,1)S(1)}, u32[]{:S(2)}, u32[]{:S(2)}) %collective-permute-start.13) | collective-permute-done | bytes 131104 | tf_op jit(solution)/shard_map/ppermute | solution.py:22
  116.7 0.8 collective-permute-start.14
  117.5 1.4 %collective-permute-done.18 = bf16[32,2,8,128]{3,2,0,1:T(8,128)(2,1)S(1)} collective-permute-done((bf16[32,2,8,128]{3,2,0,1:T(8,128)(2,1)S(1)}, bf16[32,2,8,128]{3,2,0,1:T(8,128)(2,1)S(1)}, u32[]{:S(2)}, u32[]{:S(2)}) %collective-permute-start.18) | collective-permute-done | bytes 131104 | tf_op jit(solution)/shard_map/ppermute | solution.py:22
  118.9 0.9 collective-permute-start.19
  119.9 3.8 %collective-permute-done.14 = bf16[32,8,128]{2,1,0:T(8,128)(2,1)S(1)} collective-permute-done((bf16[32,8,128]{2,1,0:T(8,128)(2,1)S(1)}, bf16[32,8,128]{2,1,0:T(8,128)(2,1)S(1)}, u32[]{:S(2)}, u32[]{:S(2)}) %collective-permute-start.14) | collective-permute-done | bytes 65568 | tf_op jit(solution)/shard_map/ppermute | solution.py:22
  123.8 1.4 %collective-permute-done.19 = bf16[32,8,128]{2,1,0:T(8,128)(2,1)S(1)} collective-permute-done((bf16[32,8,128]{2,1,0:T(8,128)(2,1)S(1)}, bf16[32,8,128]{2,1,0:T(8,128)(2,1)S(1)}, u32[]{:S(2)}, u32[]{:S(2)}) %collective-permute-start.19) | collective-permute-done | bytes 65568 | tf_op jit(solution)/shard_map/ppermute | solution.py:22
  125.2 0.8 pad_maximum_fusion.wave_ref
  126.0 3.8 %intensity.1 = f32[4,128,128]{2,1,0:T(8,128)} custom-call(f32[128,8,128]{2,1,0:T(8,128)} %pad_maximum_fusion.wave_ref, f32[256,256]{1,0:T(8,128)} %get-tuple-element.38.right_ref, f32[256,256]{1,0:T(8,128)} %get-tuple-element.37.left_ref), custom_call_target="tpu_custom_call" | custom-call | tf_op jit(solution)/shard_map/intensity/pallas_call | solution.py:174
  (102 shorter events, 6.3 us)
Async XLA Ops:
  21.7 45.6 %collective-permute-start = (bf16[32,8,16,128]{3,2,1,0:T(8,128)(2,1)S(1)}, bf16[32,8,16,128]{3,2,1,0:T(8,128)(2,1)S(1)}, u32[]{:S(2)}, u32[]{:S(2)}) collective-permute-start(bf16[32,8,16,128]{3,2,1,0:T(8,128)(2,1)S(1)} %get-tuple-element.14), channel_id=1, source_target_pairs={{0,1},{1,0},{2,3},{3,2},{4,5},{5,4},{6,7},{7,6},{8,9},{9,8},{10,11... | collective-permute-start | bytes 3145736 | tf_op jit(solution)/shard_map/ppermute | solution.py:22
  35.8 34.9 %collective-permute-start.5 = (bf16[32,8,16,128]{3,2,1,0:T(8,128)(2,1)S(1)}, bf16[32,8,16,128]{3,2,1,0:T(8,128)(2,1)S(1)}, u32[]{:S(2)}, u32[]{:S(2)}) collective-permute-start(bf16[32,8,16,128]{3,2,1,0:T(8,128)(2,1)S(1)} %get-tuple-element.16), channel_id=1, source_target_pairs={{0,1},{1,0},{2,3},{3,2},{4,5},{5,4},{6,7},{7,6},{8,9},{9,8},{10,11... | collective-permute-start | bytes 3145736 | tf_op jit(solution)/shard_map/ppermute | solution.py:22
  49.6 23.2 %collective-permute-start.10 = (bf16[32,8,16,128]{3,2,1,0:T(8,128)(2,1)S(1)}, bf16[32,8,16,128]{3,2,1,0:T(8,128)(2,1)S(1)}, u32[]{:S(2)}, u32[]{:S(2)}) collective-permute-start(bf16[32,8,16,128]{3,2,1,0:T(8,128)(2,1)S(1)} %get-tuple-element.18), channel_id=1, source_target_pairs={{0,1},{1,0},{2,3},{3,2},{4,5},{5,4},{6,7},{7,6},{8,9},{9,8},{10,11... | collective-permute-start | bytes 3145736 | tf_op jit(solution)/shard_map/ppermute | solution.py:22
  64.1 10.1 %collective-permute-start.15 = (bf16[32,8,16,128]{3,2,1,0:T(8,128)(2,1)S(1)}, bf16[32,8,16,128]{3,2,1,0:T(8,128)(2,1)S(1)}, u32[]{:S(2)}, u32[]{:S(2)}) collective-permute-start(bf16[32,8,16,128]{3,2,1,0:T(8,128)(2,1)S(1)} %get-tuple-element.20), channel_id=1, source_target_pairs={{0,1},{1,0},{2,3},{3,2},{4,5},{5,4},{6,7},{7,6},{8,9},{9,8},{10,11... | collective-permute-start | bytes 3145736 | tf_op jit(solution)/shard_map/ppermute | solution.py:22
  67.6 15.8 %collective-permute-start.1 = (bf16[32,2,2,2,8,128]{5,4,0,1,2,3:T(8,128)(2,1)S(1)}, bf16[32,2,2,2,8,128]{5,4,0,1,2,3:T(8,128)(2,1)S(1)}, u32[]{:S(2)}, u32[]{:S(2)}) collective-permute-start(bf16[32,2,2,2,8,128]{5,4,0,1,2,3:T(8,128)(2,1)S(1)} %fusion), channel_id=1, source_target_pairs={{0,4},{4,0},{8,12},{12,8},{16,20},{20,16},{24,28},{28,24},{1,5},{5... | collective-permute-start | bytes 1572872 | tf_op jit(solution)/shard_map/ppermute | solution.py:22
  71.2 14.9 %collective-permute-start.6 = (bf16[32,2,2,2,8,128]{5,4,0,1,2,3:T(8,128)(2,1)S(1)}, bf16[32,2,2,2,8,128]{5,4,0,1,2,3:T(8,128)(2,1)S(1)}, u32[]{:S(2)}, u32[]{:S(2)}) collective-permute-start(bf16[32,2,2,2,8,128]{5,4,0,1,2,3:T(8,128)(2,1)S(1)} %fusion.1), channel_id=1, source_target_pairs={{0,2},{1,3},{2,0},{3,1},{4,6},{5,7},{6,4},{7,5},{8,10},{9,11},{10,... | collective-permute-start | bytes 1572872 | tf_op jit(solution)/shard_map/ppermute | solution.py:22
  73.4 21.3 %collective-permute-start.11 = (bf16[32,2,2,2,8,128]{5,4,0,1,2,3:T(8,128)(2,1)S(1)}, bf16[32,2,2,2,8,128]{5,4,0,1,2,3:T(8,128)(2,1)S(1)}, u32[]{:S(2)}, u32[]{:S(2)}) collective-permute-start(bf16[32,2,2,2,8,128]{5,4,0,1,2,3:T(8,128)(2,1)S(1)} %fusion.2), channel_id=1, source_target_pairs={{0,4},{4,0},{8,12},{12,8},{16,20},{20,16},{24,28},{28,24},{1,5},{5... | collective-permute-start | bytes 1572872 | tf_op jit(solution)/shard_map/ppermute | solution.py:22
  74.7 22.6 %collective-permute-start.16 = (bf16[32,2,2,2,8,128]{5,4,0,1,2,3:T(8,128)(2,1)S(1)}, bf16[32,2,2,2,8,128]{5,4,0,1,2,3:T(8,128)(2,1)S(1)}, u32[]{:S(2)}, u32[]{:S(2)}) collective-permute-start(bf16[32,2,2,2,8,128]{5,4,0,1,2,3:T(8,128)(2,1)S(1)} %fusion.3), channel_id=1, source_target_pairs={{0,2},{1,3},{2,0},{3,1},{4,6},{5,7},{6,4},{7,5},{8,10},{9,11},{10,... | collective-permute-start | bytes 1572872 | tf_op jit(solution)/shard_map/ppermute | solution.py:22
  83.5 19.4 %collective-permute-start.2 = (bf16[32,2,2,8,128]{4,3,0,1,2:T(8,128)(2,1)S(1)}, bf16[32,2,2,8,128]{4,3,0,1,2:T(8,128)(2,1)S(1)}, u32[]{:S(2)}, u32[]{:S(2)}) collective-permute-start(bf16[32,2,2,8,128]{4,3,0,1,2:T(8,128)(2,1)S(1)} %fusion.6), channel_id=1, source_target_pairs={{0,2},{1,3},{2,0},{3,1},{4,6},{5,7},{6,4},{7,5},{8,10},{9,11},{10,... | collective-permute-start | bytes 786440 | tf_op jit(solution)/shard_map/ppermute | solution.py:22
  86.2 18.5 %collective-permute-start.7 = (bf16[32,2,2,8,128]{4,3,0,1,2:T(8,128)(2,1)S(1)}, bf16[32,2,2,8,128]{4,3,0,1,2:T(8,128)(2,1)S(1)}, u32[]{:S(2)}, u32[]{:S(2)}) collective-permute-start(bf16[32,2,2,8,128]{4,3,0,1,2:T(8,128)(2,1)S(1)} %fusion.7), channel_id=1, source_target_pairs={{0,4},{4,0},{8,12},{12,8},{16,20},{20,16},{24,28},{28,24},{1,5},{5... | collective-permute-start | bytes 786440 | tf_op jit(solution)/shard_map/ppermute | solution.py:22
  94.8 12.5 %collective-permute-start.12 = (bf16[32,2,2,8,128]{4,3,0,1,2:T(8,128)(2,1)S(1)}, bf16[32,2,2,8,128]{4,3,0,1,2:T(8,128)(2,1)S(1)}, u32[]{:S(2)}, u32[]{:S(2)}) collective-permute-start(bf16[32,2,2,8,128]{4,3,0,1,2:T(8,128)(2,1)S(1)} %fusion.8), channel_id=1, source_target_pairs={{0,2},{1,3},{2,0},{3,1},{4,6},{5,7},{6,4},{7,5},{8,10},{9,11},{10,... | collective-permute-start | bytes 786440 | tf_op jit(solution)/shard_map/ppermute | solution.py:22
  97.4 11.6 %collective-permute-start.17 = (bf16[32,2,2,8,128]{4,3,0,1,2:T(8,128)(2,1)S(1)}, bf16[32,2,2,8,128]{4,3,0,1,2:T(8,128)(2,1)S(1)}, u32[]{:S(2)}, u32[]{:S(2)}) collective-permute-start(bf16[32,2,2,8,128]{4,3,0,1,2:T(8,128)(2,1)S(1)} %fusion.9), channel_id=1, source_target_pairs={{0,4},{4,0},{8,12},{12,8},{16,20},{20,16},{24,28},{28,24},{1,5},{5... | collective-permute-start | bytes 786440 | tf_op jit(solution)/shard_map/ppermute | solution.py:22
  103.0 6.7 %collective-permute-start.3 = (bf16[32,2,8,128]{3,2,0,1:T(8,128)(2,1)S(1)}, bf16[32,2,8,128]{3,2,0,1:T(8,128)(2,1)S(1)}, u32[]{:S(2)}, u32[]{:S(2)}) collective-permute-start(bf16[32,2,8,128]{3,2,0,1:T(8,128)(2,1)S(1)} %fusion.10), channel_id=1, source_target_pairs={{0,8},{4,12},{8,0},{12,4},{16,24},{20,28},{24,16},{28,20},{1,9},{5... | collective-permute-start | bytes 393224 | tf_op jit(solution)/shard_map/ppermute | solution.py:22
  104.7 7.7 %collective-permute-start.8 = (bf16[32,2,8,128]{3,2,0,1:T(8,128)(2,1)S(1)}, bf16[32,2,8,128]{3,2,0,1:T(8,128)(2,1)S(1)}, u32[]{:S(2)}, u32[]{:S(2)}) collective-permute-start(bf16[32,2,8,128]{3,2,0,1:T(8,128)(2,1)S(1)} %fusion.11), channel_id=1, source_target_pairs={{0,8},{4,12},{8,0},{12,4},{16,24},{20,28},{24,16},{28,20},{1,9},{5... | collective-permute-start | bytes 393224 | tf_op jit(solution)/shard_map/ppermute | solution.py:22
  107.4 9.2 %collective-permute-start.13 = (bf16[32,2,8,128]{3,2,0,1:T(8,128)(2,1)S(1)}, bf16[32,2,8,128]{3,2,0,1:T(8,128)(2,1)S(1)}, u32[]{:S(2)}, u32[]{:S(2)}) collective-permute-start(bf16[32,2,8,128]{3,2,0,1:T(8,128)(2,1)S(1)} %fusion.12), channel_id=1, source_target_pairs={{0,8},{4,12},{8,0},{12,4},{16,24},{20,28},{24,16},{28,20},{1,9},{5... | collective-permute-start | bytes 393224 | tf_op jit(solution)/shard_map/ppermute | solution.py:22
  109.1 9.8 %collective-permute-start.18 = (bf16[32,2,8,128]{3,2,0,1:T(8,128)(2,1)S(1)}, bf16[32,2,8,128]{3,2,0,1:T(8,128)(2,1)S(1)}, u32[]{:S(2)}, u32[]{:S(2)}) collective-permute-start(bf16[32,2,8,128]{3,2,0,1:T(8,128)(2,1)S(1)} %fusion.13), channel_id=1, source_target_pairs={{0,8},{4,12},{8,0},{12,4},{16,24},{20,28},{24,16},{28,20},{1,9},{5... | collective-permute-start | bytes 393224 | tf_op jit(solution)/shard_map/ppermute | solution.py:22
  109.8 10.0 %collective-permute-start.4 = (bf16[32,8,128]{2,1,0:T(8,128)(2,1)S(1)}, bf16[32,8,128]{2,1,0:T(8,128)(2,1)S(1)}, u32[]{:S(2)}, u32[]{:S(2)}) collective-permute-start(bf16[32,8,128]{2,1,0:T(8,128)(2,1)S(1)} %fusion.19), channel_id=1, source_target_pairs={{0,16},{4,20},{8,24},{12,28},{16,0},{20,4},{24,8},{28,12},{1,17},{... | collective-permute-start | bytes 196616 | tf_op jit(solution)/shard_map/ppermute | solution.py:22
  112.4 7.4 %collective-permute-start.9 = (bf16[32,8,128]{2,1,0:T(8,128)(2,1)S(1)}, bf16[32,8,128]{2,1,0:T(8,128)(2,1)S(1)}, u32[]{:S(2)}, u32[]{:S(2)}) collective-permute-start(bf16[32,8,128]{2,1,0:T(8,128)(2,1)S(1)} %fusion.20), channel_id=1, source_target_pairs={{0,16},{4,20},{8,24},{12,28},{16,0},{20,4},{24,8},{28,12},{1,17},{... | collective-permute-start | bytes 196616 | tf_op jit(solution)/shard_map/ppermute | solution.py:22
  116.7 7.0 %collective-permute-start.14 = (bf16[32,8,128]{2,1,0:T(8,128)(2,1)S(1)}, bf16[32,8,128]{2,1,0:T(8,128)(2,1)S(1)}, u32[]{:S(2)}, u32[]{:S(2)}) collective-permute-start(bf16[32,8,128]{2,1,0:T(8,128)(2,1)S(1)} %fusion.21), channel_id=1, source_target_pairs={{0,16},{4,20},{8,24},{12,28},{16,0},{20,4},{24,8},{28,12},{1,17},{... | collective-permute-start | bytes 196616 | tf_op jit(solution)/shard_map/ppermute | solution.py:22
  118.9 6.2 %collective-permute-start.19 = (bf16[32,8,128]{2,1,0:T(8,128)(2,1)S(1)}, bf16[32,8,128]{2,1,0:T(8,128)(2,1)S(1)}, u32[]{:S(2)}, u32[]{:S(2)}) collective-permute-start(bf16[32,8,128]{2,1,0:T(8,128)(2,1)S(1)} %fusion.22), channel_id=1, source_target_pairs={{0,16},{4,20},{8,24},{12,28},{16,0},{20,4},{24,8},{28,12},{1,17},{... | collective-permute-start | bytes 196616 | tf_op jit(solution)/shard_map/ppermute | solution.py:22

commit v2 on v0

v2 whole, which is shorter than its diff:
```python
import functools
import math

import jax
import jax.numpy as jnp
import numpy as np
from jax import lax
from jax.experimental import pallas as pl
from jax.experimental.pallas import tpu as pltpu
from jax.sharding import PartitionSpec as P


BEAMS = 2048
CROP = 128
POS_DEV = 16
ROWS = 8
CHUNKS = (32, 32, 32, 32)
FIRST = "xyxy"

two_pi = 2.0 * math.pi


def exchanged(value, axis, bit):
    count = lax.axis_size(axis)
    return lax.ppermute(value, axis, [(i, i ^ bit) for i in range(count)])


def waves_kernel(tiles, beams, groups, plan, first_step, tile_ref, *refs):
    s_refs = refs[: groups * groups]
    w_ref, block_ref, low_ref, keep_ref, send_ref, rows_ref, edge_ref = refs[groups * groups :]
    strip = groups * CROP // tiles
    reach = CROP // strip
    per_owner = 2 * POS_DEV
    base_row = (pl.program_id(0) + first_step) * ROWS
    strip_at = base_row // strip
    row_in_strip = base_row % strip
    turns = groups
    own_tile = tile_ref[0]
    half = per_owner // 2
    piece = per_owner // beams
    count = (reach + 1) * per_owner

    def destinations(owner):
        place = (owner % tiles) ^ own_tile
        found = []
        for j in range(beams // 2):
            index = 0
            for axis, bit in plan:
                on = (place // bit) % 2 if axis == "tile" else j // (bit // 2) % 2
                index = 2 * index + on
            found.append(index)
        return found

    def store(r, found, part):
        part = part.astype(jnp.bfloat16)
        for j, index in enumerate(found):
            keep_ref[index, r] = part[j * piece : (j + 1) * piece]
            send_ref[index, r] = part[half + j * piece : half + (j + 1) * piece]

    def store_edge(r, found, start, began, ended):
        low = low_ref[pl.ds(start, per_owner), :]
        store(r, found, jnp.where(low <= row_in_strip + r, began, ended))

    for k in range(turns):
        for c in range(groups):
            rows_ref[k, c] = jnp.swapaxes(s_refs[k * groups + c][...], 0, 1)
        start = pl.multiple_of((reach * k + strip_at) * per_owner, per_owner)
        found = [destinations(reach * (k - 1) + strip_at + e) for e in range(reach)]
        for r in range(ROWS):
            values = jnp.concatenate([rows_ref[k, c, r] for c in range(groups)], axis=1)
            out = jnp.dot(
                w_ref[pl.ds(start, count), :], values, preferred_element_type=jnp.float32
            )
            block = block_ref[pl.ds(start, count), :]
            folded = out[:, (groups - 1) * CROP :]
            for c in range(groups - 1):
                folded = jnp.where(block == c, out[:, c * CROP : (c + 1) * CROP], folded)
            for e in range(1, reach):
                store(r, found[e], folded[e * per_owner : (e + 1) * per_owner])
            if k == 0:
                edge_ref[0, r] = folded[:per_owner]
            else:
                store_edge(r, found[0], start, edge_ref[1, r], folded[:per_owner])
            edge_ref[1, r] = folded[reach * per_owner :]
    found = destinations(reach * (turns - 1) + strip_at)
    for r in range(ROWS):
        first = pl.multiple_of(strip_at * per_owner, per_owner)
        store_edge(r, found, first, edge_ref[1, r], edge_ref[0, r])


def partial_waves(chunk, plan, smatrix, own_tile, weights, block, low):
    planes, group, field, _ = smatrix.shape
    tiles = lax.axis_size("tile")
    rows = CHUNKS[chunk]
    steps = rows // ROWS
    turns = field // CROP
    viewed = smatrix.reshape(planes * group, field, field)
    beams = lax.axis_size("beam")
    places = tiles * beams // 2
    piece = 2 * POS_DEV // beams
    shape = jax.ShapeDtypeStruct((places, rows, piece, CROP), jnp.bfloat16)
    out_spec = pl.BlockSpec((places, ROWS, piece, CROP), lambda i, t: (0, i, 0, 0))
    whole = pl.BlockSpec(memory_space=pltpu.VMEM)
    first_step = sum(CHUNKS[:chunk]) // ROWS
    flops = 2 * 3 * 2 * POS_DEV * planes * group * field * field * rows // CROP
    return pl.pallas_call(
        functools.partial(waves_kernel, tiles, beams, turns, plan, first_step),
        out_shape=(shape, shape),
        grid_spec=pltpu.PrefetchScalarGridSpec(
            num_scalar_prefetch=1,
            grid=(steps,),
            in_specs=[
                *[
                    pl.BlockSpec(
                        (planes * group, ROWS, CROP),
                        functools.partial(lambda k, c, i, t: (0, k * (CROP // ROWS) + i + first_step, c), k, c),
                    )
                    for k in range(turns)
                    for c in range(turns)
                ],
                whole,
                whole,
                whole,
            ],
            out_specs=(out_spec, out_spec),
            scratch_shapes=[
                pltpu.VMEM((turns, turns, ROWS, planes * group, CROP), jnp.bfloat16),
                pltpu.VMEM((2, ROWS, 2 * POS_DEV, CROP), jnp.float32),
            ],
        ),
        compiler_params=pltpu.CompilerParams(vmem_limit_bytes=48 * 1024 * 1024),
        cost_estimate=pl.CostEstimate(
            flops=flops,
            bytes_accessed=smatrix.size * 2 * rows // CROP,
            transcendentals=0,
        ),
    )(own_tile, *[viewed] * (turns * turns), weights, block, low)


def halves_of(value):
    high = value.astype(jnp.bfloat16)
    return high, (value - high.astype(jnp.float32)).astype(jnp.bfloat16)


def split_dot(a, b):
    dot = functools.partial(jnp.dot, preferred_element_type=jnp.float32)
    return dot(a[0], b[0]) + (dot(a[0], b[1]) + dot(a[1], b[0]))


def intensity_kernel(share, counts, right_ref, left_ref, *refs):
    *wave_refs, out_ref, rows_ref = refs
    begin = 0
    for count in counts:
        terms = [wave_refs.pop(0)[0].astype(jnp.float32) for _ in range(count)]
        total = functools.reduce(jnp.add, terms)
        size = total.shape[0] * 2 * share
        rows_ref[pl.ds(begin, size), :] = total.reshape(size, CROP)
        begin += size
    right, left = halves_of(right_ref[...]), halves_of(left_ref[...])
    begin = 0
    for wave_ref in wave_refs:
        size = wave_ref.shape[0] * 2 * share
        rows_ref[pl.ds(begin, size), :] = wave_ref[...].reshape(size, CROP)
        begin += size
    for q in range(share):
        real = rows_ref[pl.ds(2 * q, CROP, stride=2 * share), :]
        imag = rows_ref[pl.ds(2 * q + 1, CROP, stride=2 * share), :]
        joined = jnp.concatenate([real, imag], axis=1)
        halves = split_dot(halves_of(joined), right)
        halves = jnp.concatenate([halves[:, :CROP], halves[:, CROP:]], axis=0)
        full = split_dot(left, halves_of(halves))
        full_re, full_im = full[:CROP], full[CROP:]
        out_ref[q] = full_re * full_re + full_im * full_im


def intensities(sums, share):
    counts = tuple(len(terms) for terms in sums)
    waves = [term for terms in sums for term in terms]
    places = np.arange(CROP)
    angle = two_pi * (places[:, None] * places[None, :] % CROP) / CROP
    table_re = np.cos(angle) / math.sqrt(CROP)
    table_im = -np.sin(angle) / math.sqrt(CROP)
    right = np.block([[table_re, table_im], [-table_im, table_re]]).astype(np.float32)
    left = np.block([[table_re, -table_im], [table_im, table_re]]).astype(np.float32)
    return pl.pallas_call(
        functools.partial(intensity_kernel, share, counts),
        out_shape=jax.ShapeDtypeStruct((share, CROP, CROP), jnp.float32),
        grid=(1,),
        in_specs=[pl.BlockSpec((2 * CROP, 2 * CROP), lambda i: (0, 0))] * 2
        + [
            pl.BlockSpec(
                (1, rows, t.shape[2], CROP), functools.partial(lambda at, i: (0, at, 0, 0), begin // rows)
            )
            for t, begin, rows in waves
        ],
        out_specs=pl.BlockSpec((share, CROP, CROP), lambda i: (0, 0, 0)),
        scratch_shapes=[pltpu.VMEM((CROP * 2 * share, CROP), jnp.float32)],
        name="intensity",
    )(right, left, *[t for t, _, _ in waves])


def local(smatrix, offset_y, offset_x, beam_qx, beam_qy, beam_amp, beam_phase):
    tiles = lax.axis_size("tile")
    beams = lax.axis_size("beam")
    own_tile = lax.axis_index("tile")
    own_group = lax.axis_index("beam")
    planes, group, field, _ = smatrix.shape
    strip = field // tiles
    reach = CROP // strip
    share = POS_DEV // beams

    per_owner = 2 * POS_DEV
    row = jnp.arange((tiles + reach) * per_owner, dtype=jnp.int32)
    place = row % per_owner // (2 * share)
    target = (place % (beams // 2) * 2 + place // (beams // 2)) ^ own_group
    owner = (row // per_owner + tiles - reach) % tiles
    position = (owner * beams + target) * share + row // 2 % share
    listed = jnp.arange(offset_y.shape[0], dtype=jnp.int32)
    hit = position[:, None] == listed[None, :]
    first_y = jnp.sum(jnp.where(hit, offset_y[None, :], 0), axis=1, dtype=jnp.int32)[:, None]
    first_x = jnp.sum(jnp.where(hit, offset_x[None, :], 0), axis=1, dtype=jnp.int32)[:, None]

    table = jnp.stack(
        [beam_qx.astype(jnp.float32), beam_qy.astype(jnp.float32), beam_amp, beam_phase]
    )
    table = lax.dynamic_slice_in_dim(table, own_tile * group, group, 1)
    table = jnp.concatenate([table, table], axis=1)
    qx, qy = table[0:1].astype(jnp.int32), table[1:2].astype(jnp.int32)
    scale = table[2:3] * (1.0 / math.sqrt(BEAMS))
    turns = ((first_x + CROP // 2) * qx + (first_y + CROP // 2) * qy) % field
    angle = table[3:4] - two_pi * turns.astype(jnp.float32) / field
    w_real, w_imag = scale * jnp.cos(angle), scale * jnp.sin(angle)
    imag_out = (row % 2 == 1)[:, None]
    imag_in = (jnp.arange(planes * group, dtype=jnp.int32) >= group)[None, :]
    weights = jnp.where(
        imag_out == imag_in, w_real, jnp.where(imag_out, w_imag, -w_imag)
    ).astype(jnp.bfloat16)
    lanes = jnp.arange(CROP, dtype=jnp.int32)[None, :]
    block = (first_x // CROP + (lanes < first_x % CROP).astype(jnp.int32)) % (field // CROP)
    low = jnp.broadcast_to(first_y % strip, block.shape)
    own = own_tile.reshape(1).astype(jnp.int32)

    tile_bits = [1 << b for b in range(tiles.bit_length() - 1)]
    beam_bits = [1 << b for b in range(beams.bit_length() - 1)]
    near = [("tile", tile_bits[0])]
    rest = [("tile", b) for b in tile_bits[1:]]
    beside = [("beam", b) for b in beam_bits[1:]]
    sums = []
    for chunk in range(len(CHUNKS)):
        plan = near + beside if FIRST[chunk] == "x" else beside + near
        keep, send = partial_waves(
            chunk, tuple(plan + rest), smatrix, own, weights, block, low
        )
        arrived = exchanged(send, "beam", 1)
        rows = CHUNKS[chunk]
        terms = [(keep, 0, rows), (arrived, 0, rows)]
        count = keep.shape[0]
        for name in plan:
            count //= 2
            terms = halved([terms], name, count)[0]
        sums.append(terms)
    for first in range(len(CHUNKS)):
        pair = sums[first : first + 1]
        left = count
        for name in rest:
            left //= 2
            pair = halved(pair, name, left)
        sums[first : first + 1] = pair
    return intensities(sums, share)


def halved(sums, name, count):
    packed = []
    for terms in sums:
        away = [
            t[count : 2 * count, begin : begin + rows].astype(jnp.float32)
            for t, begin, rows in terms
        ]
        packed.append(functools.reduce(jnp.add, away).astype(jnp.bfloat16))
    packed = packed[0] if len(packed) == 1 else jnp.concatenate(packed, axis=1)
    arrived = exchanged(packed, *name)
    result, begin = [], 0
    for terms in sums:
        rows = terms[0][2]
        result.append(terms + [(arrived, begin, rows)])
        begin += rows
    return result


def solution(mesh):
    return jax.shard_map(
        local,
        mesh=mesh,
        in_specs=(
            P(None, ("beam", "tile"), None, None),
            P(),
            P(),
            P("beam"),
            P("beam"),
            P("beam"),
            P("beam"),
        ),
        out_specs=P(("tile", "beam"), None, None),
        check_vma=False,
    )
```

time: 1900 us -> 118 us (0.06)
  waiting for transfers between devices: 1480 us -> 24.7 us
  local copies, waits for them, and re-layouts: 253 us -> 0.78 us
  matrix products: 72.2 us -> 0 us
  Pallas kernels: 0 us -> 48.6 us
  other arithmetic: 66 us -> 18 us
    all_to_all x1 -> x0, waiting for transfers between devices: 1440 us -> none  [local(): lax.all_to_all(smatrix, 'tile', split_axis=2, concat_axis=1, tiled=True)]
    unnamed x25 -> x42, local copies, waits for them, and re-layouts: 125 us -> 0.69 us
    dot_general x5 -> x0, matrix products: 72.2 us -> none  [the longest x3 71 us: owner_block(): jnp.dot(mixing, stacked, preferred_element_type=jnp.float32)]
    all_to_all x1 -> x0, local copies, waits for them, and re-layouts: 59.8 us -> none  [local(): lax.all_to_all(smatrix, 'tile', split_axis=2, concat_axis=1, tiled=True)]
    concatenate x4 -> x1, other arithmetic: 54.8 us -> 0.08 us  [local(): table = jnp.concatenate([table, table], axis=1)]
    pallas_call x0 -> x5, Pallas kernels: none -> 48.6 us  [the longest x4 44.6 us: partial_waves(): pl.pallas_call(functools.partial(waves_kernel, tiles, beams, turns, plan,...]
    reshape x8 -> x0, local copies, waits for them, and re-layouts: 33.6 us -> none  [the longest x3 32.8 us: owner_block(): waves = waves.reshape(POS_DEV, 2, strip, field)]
    reduce_scatter x1 -> x0, waiting for transfers between devices: 27.1 us -> none  [local(): lax.psum_scatter(blocks.astype(jnp.float32).astype(jnp.bfloat16), 'beam',...]
  transfers between devices with their start and end apart: 4 -> 20, of which waited for: 4 -> 9; matrix products, arithmetic and copies ran while one was open for 0% -> 12% of each run, Pallas kernels for 0% -> 28%
where the time goes in v2:
time: 118 us; the launch traced here: 117 us
  Pallas kernels  48.6 us (41%)
  waiting for transfers between devices  24.7 us (21%)
  starting transfers between devices  24.4 us (21%)
  other arithmetic  18 us (15%)
    pallas_call x4, Pallas kernels, partial_waves(): pl.pallas_call(functools.partial(waves_kernel, tiles, beams, turns, plan,...  44.6 us
    ppermute x20, waiting for transfers between devices, exchanged(): return lax.ppermute(value, axis, [(i, i ^ bit) for i in range(count)])  24.7 us
    ppermute x20, starting transfers between devices, exchanged(): return lax.ppermute(value, axis, [(i, i ^ bit) for i in range(count)])  24.4 us
    convert_element_type x16, other arithmetic, halved(): packed.append(functools.reduce(jnp.add, away).astype(jnp.bfloat16))  13.6 us
    pallas_call x1, Pallas kernels, intensities(): pl.pallas_call(functools.partial(intensity_kernel, share, counts), out_sh...  4 us
  transfers between devices with their start and end apart: 20, of which 9 were waited for; matrix products, arithmetic and copies ran while one was open for 12% of the time, Pallas kernels for 28%

profile of v2, /device:TPU:0, one launch (start us, length us, event | category | flops | bytes accessed | tf_op | source)
XLA Modules:
  0.0 116.8 jit_solution(14717560359730464014)
XLA Ops:
  0.0 0.7 convert_element_type.237
  0.7 0.7 convert_element_type.238
  1.4 0.7 fusion.27
  2.2 1.0 select_reduce_fusion.1
  3.4 1.0 fusion.5.refs_16_
  4.5 11.4 %shard_map.94 = (bf16[16,32,8,128]{3,2,1,0:T(8,128)(2,1)S(1)}, bf16[16,32,8,128]{3,2,1,0:T(8,128)(2,1)}) custom-call(s32[1]{0:T(128)} %bitcast.tile_ref, bf16[128,512,512]{2,1,0:T(8,128)(2,1)} %bitcast.1.refs_0_.refs_1_.refs_2_.refs_3_.refs_4_.refs_5_.refs_6_.refs_7_.refs_8_.refs_9_.refs_10_.refs_11_.refs_12_.refs_13_.refs_14_.refs_15_, ...), custom_call_target="tpu_custom_call" | custom-call | flops 1610612736 | bytes 16777216 | tf_op jit(solution)/shard_map/pallas_call | solution.py:106
  15.9 0.6 collective-permute-start.15
  16.4 11.3 %shard_map.93 = (bf16[16,32,8,128]{3,2,1,0:T(8,128)(2,1)S(1)}, bf16[16,32,8,128]{3,2,1,0:T(8,128)(2,1)}) custom-call(s32[1]{0:T(128)} %bitcast.tile_ref, bf16[128,512,512]{2,1,0:T(8,128)(2,1)} %bitcast.1.refs_0_.refs_1_.refs_2_.refs_3_.refs_4_.refs_5_.refs_6_.refs_7_.refs_8_.refs_9_.refs_10_.refs_11_.refs_12_.refs_13_.refs_14_.refs_15_, ...), custom_call_target="tpu_custom_call" | custom-call | flops 1610612736 | bytes 16777216 | tf_op jit(solution)/shard_map/pallas_call | solution.py:106
  27.7 0.3 collective-permute-start.10
  28.1 11.3 %shard_map.92 = (bf16[16,32,8,128]{3,2,1,0:T(8,128)(2,1)S(1)}, bf16[16,32,8,128]{3,2,1,0:T(8,128)(2,1)}) custom-call(s32[1]{0:T(128)} %bitcast.tile_ref, bf16[128,512,512]{2,1,0:T(8,128)(2,1)} %bitcast.1.refs_0_.refs_1_.refs_2_.refs_3_.refs_4_.refs_5_.refs_6_.refs_7_.refs_8_.refs_9_.refs_10_.refs_11_.refs_12_.refs_13_.refs_14_.refs_15_, ...), custom_call_target="tpu_custom_call" | custom-call | flops 1610612736 | bytes 16777216 | tf_op jit(solution)/shard_map/pallas_call | solution.py:106
  39.7 10.6 %shard_map.91 = (bf16[16,32,8,128]{3,2,1,0:T(8,128)(2,1)S(1)}, bf16[16,32,8,128]{3,2,1,0:T(8,128)(2,1)S(1)}) custom-call(s32[1]{0:T(128)} %bitcast.tile_ref, bf16[128,512,512]{2,1,0:T(8,128)(2,1)} %bitcast.1.refs_0_.refs_1_.refs_2_.refs_3_.refs_4_.refs_5_.refs_6_.refs_7_.refs_8_.refs_9_.refs_10_.refs_11_.refs_12_.refs_13_.refs_14_.refs_15_, ...), custom_call_target="tpu_custom_call" | custom-call | flops 1610612736 | bytes 16777216 | tf_op jit(solution)/shard_map/pallas_call | solution.py:106
  50.7 1.2 %add_convert_fusion = bf16[8,32,8,128]{3,2,1,0:T(8,128)(2,1)S(1)} fusion(bf16[16,32,8,128]{3,2,1,0:T(8,128)(2,1)} %collective-permute-done.15.refs_19_, bf16[16,32,8,128]{3,2,1,0:T(8,128)(2,1)S(1)} %get-tuple-element.19.refs_18_), kind=kLoop, calls=%fused_computation | loop fusion | flops 1048576 | bytes 1572864 | tf_op jit(solution)/shard_map/convert_element_type | solution.py:279
  51.9 2.8 %collective-permute-start.16 = (bf16[8,32,8,128]{3,2,1,0:T(8,128)(2,1)S(1)}, bf16[8,32,8,128]{3,2,1,0:T(8,128)(2,1)S(1)}, u32[]{:S(2)}, u32[]{:S(2)}) collective-permute-start(bf16[8,32,8,128]{3,2,1,0:T(8,128)(2,1)S(1)} %add_convert_fusion), channel_id=1, source_target_pairs={{0,2},{1,3},{2,0},{3,1},{4,6},{5,7},{6,4},{7,5},{8,10},{9,11},{10,... | collective-permute-start | bytes 1572872 | tf_op jit(solution)/shard_map/ppermute | solution.py:25
  54.7 1.2 %add_convert_fusion.1 = bf16[8,32,8,128]{3,2,1,0:T(8,128)(2,1)S(1)} fusion(bf16[16,32,8,128]{3,2,1,0:T(8,128)(2,1)} %collective-permute-done.10.refs_13_, bf16[16,32,8,128]{3,2,1,0:T(8,128)(2,1)S(1)} %get-tuple-element.17.refs_12_), kind=kLoop, calls=%fused_computation.1 | loop fusion | flops 1048576 | bytes 1572864 | tf_op jit(solution)/shard_map/convert_element_type | solution.py:279
  55.9 1.6 %collective-permute-start.11 = (bf16[8,32,8,128]{3,2,1,0:T(8,128)(2,1)S(1)}, bf16[8,32,8,128]{3,2,1,0:T(8,128)(2,1)S(1)}, u32[]{:S(2)}, u32[]{:S(2)}) collective-permute-start(bf16[8,32,8,128]{3,2,1,0:T(8,128)(2,1)S(1)} %add_convert_fusion.1), channel_id=1, source_target_pairs={{0,4},{4,0},{8,12},{12,8},{16,20},{20,16},{24,28},{28,24},{1,5},{5... | collective-permute-start | bytes 1572872 | tf_op jit(solution)/shard_map/ppermute | solution.py:25
  57.5 1.2 %add_convert_fusion.2 = bf16[8,32,8,128]{3,2,1,0:T(8,128)(2,1)S(1)} fusion(bf16[16,32,8,128]{3,2,1,0:T(8,128)(2,1)} %collective-permute-done.5.refs_7_, bf16[16,32,8,128]{3,2,1,0:T(8,128)(2,1)S(1)} %get-tuple-element.15.refs_6_), kind=kLoop, calls=%fused_computation.2 | loop fusion | flops 1048576 | bytes 1572864 | tf_op jit(solution)/shard_map/convert_element_type | solution.py:279
  58.7 0.6 collective-permute-start.6
  59.5 8.0 %collective-permute-done.16.refs_20_ = bf16[8,32,8,128]{3,2,1,0:T(8,128)(2,1)S(1)} collective-permute-done((bf16[8,32,8,128]{3,2,1,0:T(8,128)(2,1)S(1)}, bf16[8,32,8,128]{3,2,1,0:T(8,128)(2,1)S(1)}, u32[]{:S(2)}, u32[]{:S(2)}) %collective-permute-start.16) | collective-permute-done | bytes 524320 | tf_op jit(solution)/shard_map/ppermute | solution.py:25
  67.5 1.2 %add_convert_fusion.4 = bf16[4,32,8,128]{3,2,1,0:T(8,128)(2,1)S(1)} fusion(bf16[8,32,8,128]{3,2,1,0:T(8,128)(2,1)S(1)} %collective-permute-done.16.refs_20_, bf16[16,32,8,128]{3,2,1,0:T(8,128)(2,1)} %collective-permute-done.15.refs_19_, bf16[16,32,8,128]{3,2,1,0:T(8,128)(2,1)S(1)} %get-tuple-element.19.refs_18_), kind=kLoop, calls=%fused_computation.4 | loop fusion | flops 786432 | bytes 1048576 | tf_op jit(solution)/shard_map/convert_element_type | solution.py:279
  68.7 2.1 %collective-permute-start.17 = (bf16[4,32,8,128]{3,2,1,0:T(8,128)(2,1)S(1)}, bf16[4,32,8,128]{3,2,1,0:T(8,128)(2,1)S(1)}, u32[]{:S(2)}, u32[]{:S(2)}) collective-permute-start(bf16[4,32,8,128]{3,2,1,0:T(8,128)(2,1)S(1)} %add_convert_fusion.4), channel_id=1, source_target_pairs={{0,4},{4,0},{8,12},{12,8},{16,20},{20,16},{24,28},{28,24},{1,5},{5... | collective-permute-start | bytes 786440 | tf_op jit(solution)/shard_map/ppermute | solution.py:25
  70.8 1.2 %add_convert_fusion.5 = bf16[4,32,8,128]{3,2,1,0:T(8,128)(2,1)S(1)} fusion(bf16[8,32,8,128]{3,2,1,0:T(8,128)(2,1)S(1)} %collective-permute-done.11.refs_14_, bf16[16,32,8,128]{3,2,1,0:T(8,128)(2,1)} %collective-permute-done.10.refs_13_, bf16[16,32,8,128]{3,2,1,0:T(8,128)(2,1)S(1)} %get-tuple-element.17.refs_12_), kind=kLoop, calls=%fused_computation.5 | loop fusion | flops 786432 | bytes 1048576 | tf_op jit(solution)/shard_map/convert_element_type | solution.py:279
  72.0 1.6 %collective-permute-start.12 = (bf16[4,32,8,128]{3,2,1,0:T(8,128)(2,1)S(1)}, bf16[4,32,8,128]{3,2,1,0:T(8,128)(2,1)S(1)}, u32[]{:S(2)}, u32[]{:S(2)}) collective-permute-start(bf16[4,32,8,128]{3,2,1,0:T(8,128)(2,1)S(1)} %add_convert_fusion.5), channel_id=1, source_target_pairs={{0,2},{1,3},{2,0},{3,1},{4,6},{5,7},{6,4},{7,5},{8,10},{9,11},{10,... | collective-permute-start | bytes 786440 | tf_op jit(solution)/shard_map/ppermute | solution.py:25
  73.6 5.1 %collective-permute-done.6.refs_8_ = bf16[8,32,8,128]{3,2,1,0:T(8,128)(2,1)S(1)} collective-permute-done((bf16[8,32,8,128]{3,2,1,0:T(8,128)(2,1)S(1)}, bf16[8,32,8,128]{3,2,1,0:T(8,128)(2,1)S(1)}, u32[]{:S(2)}, u32[]{:S(2)}) %collective-permute-start.6) | collective-permute-done | bytes 524320 | tf_op jit(solution)/shard_map/ppermute | solution.py:25
  78.7 1.2 %add_convert_fusion.6 = bf16[4,32,8,128]{3,2,1,0:T(8,128)(2,1)S(1)} fusion(bf16[8,32,8,128]{3,2,1,0:T(8,128)(2,1)S(1)} %collective-permute-done.6.refs_8_, bf16[16,32,8,128]{3,2,1,0:T(8,128)(2,1)} %collective-permute-done.5.refs_7_, bf16[16,32,8,128]{3,2,1,0:T(8,128)(2,1)S(1)} %get-tuple-element.15.refs_6_), kind=kLoop, calls=%fused_computation.6 | loop fusion | flops 786432 | bytes 1048576 | tf_op jit(solution)/shard_map/convert_element_type | solution.py:279
  80.0 2.1 %collective-permute-start.7 = (bf16[4,32,8,128]{3,2,1,0:T(8,128)(2,1)S(1)}, bf16[4,32,8,128]{3,2,1,0:T(8,128)(2,1)S(1)}, u32[]{:S(2)}, u32[]{:S(2)}) collective-permute-start(bf16[4,32,8,128]{3,2,1,0:T(8,128)(2,1)S(1)} %add_convert_fusion.6), channel_id=1, source_target_pairs={{0,4},{4,0},{8,12},{12,8},{16,20},{20,16},{24,28},{28,24},{1,5},{5... | collective-permute-start | bytes 786440 | tf_op jit(solution)/shard_map/ppermute | solution.py:25
  82.1 1.6 %collective-permute-start.2 = (bf16[4,32,8,128]{3,2,1,0:T(8,128)(2,1)S(1)}, bf16[4,32,8,128]{3,2,1,0:T(8,128)(2,1)S(1)}, u32[]{:S(2)}, u32[]{:S(2)}) collective-permute-start(bf16[4,32,8,128]{3,2,1,0:T(8,128)(2,1)S(1)} %add_convert_fusion.7), channel_id=1, source_target_pairs={{0,2},{1,3},{2,0},{3,1},{4,6},{5,7},{6,4},{7,5},{8,10},{9,11},{10,... | collective-permute-start | bytes 786440 | tf_op jit(solution)/shard_map/ppermute | solution.py:25
  83.7 3.9 %collective-permute-done.17.refs_21_ = bf16[4,32,8,128]{3,2,1,0:T(8,128)(2,1)S(1)} collective-permute-done((bf16[4,32,8,128]{3,2,1,0:T(8,128)(2,1)S(1)}, bf16[4,32,8,128]{3,2,1,0:T(8,128)(2,1)S(1)}, u32[]{:S(2)}, u32[]{:S(2)}) %collective-permute-start.17) | collective-permute-done | bytes 262176 | tf_op jit(solution)/shard_map/ppermute | solution.py:25
  87.6 1.1 add_convert_fusion.8
  88.7 1.6 %collective-permute-start.18 = (bf16[2,32,8,128]{3,2,1,0:T(8,128)(2,1)S(1)}, bf16[2,32,8,128]{3,2,1,0:T(8,128)(2,1)S(1)}, u32[]{:S(2)}, u32[]{:S(2)}) collective-permute-start(bf16[2,32,8,128]{3,2,1,0:T(8,128)(2,1)S(1)} %add_convert_fusion.8), channel_id=1, source_target_pairs={{0,8},{4,12},{8,0},{12,4},{16,24},{20,28},{24,16},{28,20},{1,9},{5... | collective-permute-start | bytes 393224 | tf_op jit(solution)/shard_map/ppermute | solution.py:25
  90.3 1.1 add_convert_fusion.9
  91.4 0.5 collective-permute-start.13
  92.2 1.1 add_convert_fusion.10
  93.3 1.6 %collective-permute-start.8 = (bf16[2,32,8,128]{3,2,1,0:T(8,128)(2,1)S(1)}, bf16[2,32,8,128]{3,2,1,0:T(8,128)(2,1)S(1)}, u32[]{:S(2)}, u32[]{:S(2)}) collective-permute-start(bf16[2,32,8,128]{3,2,1,0:T(8,128)(2,1)S(1)} %add_convert_fusion.10), channel_id=1, source_target_pairs={{0,8},{4,12},{8,0},{12,4},{16,24},{20,28},{24,16},{28,20},{1,9},{5... | collective-permute-start | bytes 393224 | tf_op jit(solution)/shard_map/ppermute | solution.py:25
  95.0 0.5 collective-permute-start.3
  95.6 0.9 add_convert_fusion.12
  96.5 2.7 %collective-permute-start.19 = (bf16[1,32,8,128]{3,2,1,0:T(8,128)(2,1)S(1)}, bf16[1,32,8,128]{3,2,1,0:T(8,128)(2,1)S(1)}, u32[]{:S(2)}, u32[]{:S(2)}) collective-permute-start(bf16[1,32,8,128]{3,2,1,0:T(8,128)(2,1)S(1)} %add_convert_fusion.12), channel_id=1, source_target_pairs={{0,16},{4,20},{8,24},{12,28},{16,0},{20,4},{24,8},{28,12},{1,17},{... | collective-permute-start | bytes 196616 | tf_op jit(solution)/shard_map/ppermute | solution.py:25
  99.2 0.9 add_convert_fusion.13
  100.1 1.3 %collective-permute-start.14 = (bf16[1,32,8,128]{3,2,1,0:T(8,128)(2,1)S(1)}, bf16[1,32,8,128]{3,2,1,0:T(8,128)(2,1)S(1)}, u32[]{:S(2)}, u32[]{:S(2)}) collective-permute-start(bf16[1,32,8,128]{3,2,1,0:T(8,128)(2,1)S(1)} %add_convert_fusion.13), channel_id=1, source_target_pairs={{0,16},{4,20},{8,24},{12,28},{16,0},{20,4},{24,8},{28,12},{1,17},{... | collective-permute-start | bytes 196616 | tf_op jit(solution)/shard_map/ppermute | solution.py:25
  101.4 1.3 %collective-permute-done.8.refs_10_ = bf16[2,32,8,128]{3,2,1,0:T(8,128)(2,1)S(1)} collective-permute-done((bf16[2,32,8,128]{3,2,1,0:T(8,128)(2,1)S(1)}, bf16[2,32,8,128]{3,2,1,0:T(8,128)(2,1)S(1)}, u32[]{:S(2)}, u32[]{:S(2)}) %collective-permute-start.8) | collective-permute-done | bytes 131104 | tf_op jit(solution)/shard_map/ppermute | solution.py:25
  102.7 0.9 add_convert_fusion.14
  103.7 0.6 collective-permute-start.9
  104.3 0.8 collective-permute-done.3.refs_4_
  105.1 1.6 %collective-permute-start.4 = (bf16[1,32,8,128]{3,2,1,0:T(8,128)(2,1)S(1)}, bf16[1,32,8,128]{3,2,1,0:T(8,128)(2,1)S(1)}, u32[]{:S(2)}, u32[]{:S(2)}) collective-permute-start(bf16[1,32,8,128]{3,2,1,0:T(8,128)(2,1)S(1)} %add_convert_fusion.15), channel_id=1, source_target_pairs={{0,16},{4,20},{8,24},{12,28},{16,0},{20,4},{24,8},{28,12},{1,17},{... | collective-permute-start | bytes 196616 | tf_op jit(solution)/shard_map/ppermute | solution.py:25
  106.8 2.7 %collective-permute-done.14.refs_17_ = bf16[1,32,8,128]{3,2,1,0:T(8,128)(2,1)S(1)} collective-permute-done((bf16[1,32,8,128]{3,2,1,0:T(8,128)(2,1)S(1)}, bf16[1,32,8,128]{3,2,1,0:T(8,128)(2,1)S(1)}, u32[]{:S(2)}, u32[]{:S(2)}) %collective-permute-start.14) | collective-permute-done | bytes 65568 | tf_op jit(solution)/shard_map/ppermute | solution.py:25
  109.5 1.9 %collective-permute-done.9.refs_11_ = bf16[1,32,8,128]{3,2,1,0:T(8,128)(2,1)S(1)} collective-permute-done((bf16[1,32,8,128]{3,2,1,0:T(8,128)(2,1)S(1)}, bf16[1,32,8,128]{3,2,1,0:T(8,128)(2,1)S(1)}, u32[]{:S(2)}, u32[]{:S(2)}) %collective-permute-start.9) | collective-permute-done | bytes 65568 | tf_op jit(solution)/shard_map/ppermute | solution.py:25
  111.5 0.6 collective-permute-done.4.refs_5_
  112.2 0.6 copy-done.20
  112.8 4.0 %intensity.1 = f32[4,128,128]{2,1,0:T(8,128)} custom-call(f32[256,256]{1,0:T(8,128)} %constant.178.clone.right_ref, f32[256,256]{1,0:T(8,128)} %constant.179.clone.left_ref, bf16[16,32,8,128]{3,2,1,0:T(8,128)(2,1)} %copy-done.3, bf16[16,32,8,128]{3,2,1,0:T(8,128)(2,1)} %copy-done.4, bf16[8,32,8,128]{3,2,1,0:T(8,128)(2,1)} %copy-done.8, ...), custom_call_target="tpu_custom_call" | custom-call | tf_op jit(solution)/shard_map/intensity/pallas_call | solution.py:185
  (68 shorter events, 1.9 us)
Async XLA Ops:
  15.9 79.7 %copy-start = (bf16[16,32,8,128]{3,2,1,0:T(8,128)(2,1)}, bf16[16,32,8,128]{3,2,1,0:T(8,128)(2,1)S(1)}, u32[]{:S(2)}) copy-start(bf16[16,32,8,128]{3,2,1,0:T(8,128)(2,1)S(1)} %get-tuple-element.19.refs_18_) | copy-start | bytes 3145732
  15.9 34.8 %collective-permute-start.15 = (bf16[16,32,8,128]{3,2,1,0:T(8,128)(2,1)}, bf16[16,32,8,128]{3,2,1,0:T(8,128)(2,1)}, u32[]{:S(2)}, u32[]{:S(2)}) collective-permute-start(bf16[16,32,8,128]{3,2,1,0:T(8,128)(2,1)} %get-tuple-element.20), channel_id=1, source_target_pairs={{0,1},{1,0},{2,3},{3,2},{4,5},{5,4},{6,7},{7,6},{8,9},{9,8},{10,11... | collective-permute-start | bytes 3145736 | tf_op jit(solution)/shard_map/ppermute | solution.py:25
  27.7 71.5 %copy-start.1 = (bf16[16,32,8,128]{3,2,1,0:T(8,128)(2,1)}, bf16[16,32,8,128]{3,2,1,0:T(8,128)(2,1)S(1)}, u32[]{:S(2)}) copy-start(bf16[16,32,8,128]{3,2,1,0:T(8,128)(2,1)S(1)} %get-tuple-element.17.refs_12_) | copy-start | bytes 3145732
  27.7 27.0 %collective-permute-start.10 = (bf16[16,32,8,128]{3,2,1,0:T(8,128)(2,1)}, bf16[16,32,8,128]{3,2,1,0:T(8,128)(2,1)}, u32[]{:S(2)}, u32[]{:S(2)}) collective-permute-start(bf16[16,32,8,128]{3,2,1,0:T(8,128)(2,1)} %get-tuple-element.18), channel_id=1, source_target_pairs={{0,1},{1,0},{2,3},{3,2},{4,5},{5,4},{6,7},{7,6},{8,9},{9,8},{10,11... | collective-permute-start | bytes 3145736 | tf_op jit(solution)/shard_map/ppermute | solution.py:25
  39.4 63.4 %copy-start.2 = (bf16[16,32,8,128]{3,2,1,0:T(8,128)(2,1)}, bf16[16,32,8,128]{3,2,1,0:T(8,128)(2,1)S(1)}, u32[]{:S(2)}) copy-start(bf16[16,32,8,128]{3,2,1,0:T(8,128)(2,1)S(1)} %get-tuple-element.15.refs_6_) | copy-start | bytes 3145732
  39.4 18.1 %collective-permute-start.5 = (bf16[16,32,8,128]{3,2,1,0:T(8,128)(2,1)}, bf16[16,32,8,128]{3,2,1,0:T(8,128)(2,1)}, u32[]{:S(2)}, u32[]{:S(2)}) collective-permute-start(bf16[16,32,8,128]{3,2,1,0:T(8,128)(2,1)} %get-tuple-element.16), channel_id=1, source_target_pairs={{0,1},{1,0},{2,3},{3,2},{4,5},{5,4},{6,7},{7,6},{8,9},{9,8},{10,11... | collective-permute-start | bytes 3145736 | tf_op jit(solution)/shard_map/ppermute | solution.py:25
  50.3 54.7 %copy-start.3 = (bf16[16,32,8,128]{3,2,1,0:T(8,128)(2,1)}, bf16[16,32,8,128]{3,2,1,0:T(8,128)(2,1)S(1)}, u32[]{:S(2)}) copy-start(bf16[16,32,8,128]{3,2,1,0:T(8,128)(2,1)S(1)} %get-tuple-element.13.refs_0_) | copy-start | bytes 3145732
  50.4 8.9 %collective-permute-start = (bf16[16,32,8,128]{3,2,1,0:T(8,128)(2,1)S(1)}, bf16[16,32,8,128]{3,2,1,0:T(8,128)(2,1)S(1)}, u32[]{:S(2)}, u32[]{:S(2)}) collective-permute-start(bf16[16,32,8,128]{3,2,1,0:T(8,128)(2,1)S(1)} %get-tuple-element.14), channel_id=1, source_target_pairs={{0,1},{1,0},{2,3},{3,2},{4,5},{5,4},{6,7},{7,6},{8,9},{9,8},{10,11... | collective-permute-start | bytes 3145736 | tf_op jit(solution)/shard_map/ppermute | solution.py:25
  51.9 15.6 %collective-permute-start.16 = (bf16[8,32,8,128]{3,2,1,0:T(8,128)(2,1)S(1)}, bf16[8,32,8,128]{3,2,1,0:T(8,128)(2,1)S(1)}, u32[]{:S(2)}, u32[]{:S(2)}) collective-permute-start(bf16[8,32,8,128]{3,2,1,0:T(8,128)(2,1)S(1)} %add_convert_fusion), channel_id=1, source_target_pairs={{0,2},{1,3},{2,0},{3,1},{4,6},{5,7},{6,4},{7,5},{8,10},{9,11},{10,... | collective-permute-start | bytes 1572872 | tf_op jit(solution)/shard_map/ppermute | solution.py:25
  55.9 14.9 %collective-permute-start.11 = (bf16[8,32,8,128]{3,2,1,0:T(8,128)(2,1)S(1)}, bf16[8,32,8,128]{3,2,1,0:T(8,128)(2,1)S(1)}, u32[]{:S(2)}, u32[]{:S(2)}) collective-permute-start(bf16[8,32,8,128]{3,2,1,0:T(8,128)(2,1)S(1)} %add_convert_fusion.1), channel_id=1, source_target_pairs={{0,4},{4,0},{8,12},{12,8},{16,20},{20,16},{24,28},{28,24},{1,5},{5... | collective-permute-start | bytes 1572872 | tf_op jit(solution)/shard_map/ppermute | solution.py:25
  58.7 20.1 %collective-permute-start.6 = (bf16[8,32,8,128]{3,2,1,0:T(8,128)(2,1)S(1)}, bf16[8,32,8,128]{3,2,1,0:T(8,128)(2,1)S(1)}, u32[]{:S(2)}, u32[]{:S(2)}) collective-permute-start(bf16[8,32,8,128]{3,2,1,0:T(8,128)(2,1)S(1)} %add_convert_fusion.2), channel_id=1, source_target_pairs={{0,2},{1,3},{2,0},{3,1},{4,6},{5,7},{6,4},{7,5},{8,10},{9,11},{10,... | collective-permute-start | bytes 1572872 | tf_op jit(solution)/shard_map/ppermute | solution.py:25
  59.2 45.9 %copy-start.4 = (bf16[16,32,8,128]{3,2,1,0:T(8,128)(2,1)}, bf16[16,32,8,128]{3,2,1,0:T(8,128)(2,1)S(1)}, u32[]{:S(2)}) copy-start(bf16[16,32,8,128]{3,2,1,0:T(8,128)(2,1)S(1)} %collective-permute-done.refs_1_) | copy-start | bytes 3145732
  59.4 22.6 %collective-permute-start.1 = (bf16[8,32,8,128]{3,2,1,0:T(8,128)(2,1)S(1)}, bf16[8,32,8,128]{3,2,1,0:T(8,128)(2,1)S(1)}, u32[]{:S(2)}, u32[]{:S(2)}) collective-permute-start(bf16[8,32,8,128]{3,2,1,0:T(8,128)(2,1)S(1)} %add_convert_fusion.3), channel_id=1, source_target_pairs={{0,4},{4,0},{8,12},{12,8},{16,20},{20,16},{24,28},{28,24},{1,5},{5... | collective-permute-start | bytes 1572872 | tf_op jit(solution)/shard_map/ppermute | solution.py:25
  67.5 39.3 %copy-start.5 = (bf16[8,32,8,128]{3,2,1,0:T(8,128)(2,1)}, bf16[8,32,8,128]{3,2,1,0:T(8,128)(2,1)S(1)}, u32[]{:S(2)}) copy-start(bf16[8,32,8,128]{3,2,1,0:T(8,128)(2,1)S(1)} %collective-permute-done.16.refs_20_) | copy-start | bytes 1572868
  68.7 18.9 %collective-permute-start.17 = (bf16[4,32,8,128]{3,2,1,0:T(8,128)(2,1)S(1)}, bf16[4,32,8,128]{3,2,1,0:T(8,128)(2,1)S(1)}, u32[]{:S(2)}, u32[]{:S(2)}) collective-permute-start(bf16[4,32,8,128]{3,2,1,0:T(8,128)(2,1)S(1)} %add_convert_fusion.4), channel_id=1, source_target_pairs={{0,4},{4,0},{8,12},{12,8},{16,20},{20,16},{24,28},{28,24},{1,5},{5... | collective-permute-start | bytes 786440 | tf_op jit(solution)/shard_map/ppermute | solution.py:25
  70.8 36.0 %copy-start.6 = (bf16[8,32,8,128]{3,2,1,0:T(8,128)(2,1)}, bf16[8,32,8,128]{3,2,1,0:T(8,128)(2,1)S(1)}, u32[]{:S(2)}) copy-start(bf16[8,32,8,128]{3,2,1,0:T(8,128)(2,1)S(1)} %collective-permute-done.11.refs_14_) | copy-start | bytes 1572868
  72.0 18.3 %collective-permute-start.12 = (bf16[4,32,8,128]{3,2,1,0:T(8,128)(2,1)S(1)}, bf16[4,32,8,128]{3,2,1,0:T(8,128)(2,1)S(1)}, u32[]{:S(2)}, u32[]{:S(2)}) collective-permute-start(bf16[4,32,8,128]{3,2,1,0:T(8,128)(2,1)S(1)} %add_convert_fusion.5), channel_id=1, source_target_pairs={{0,2},{1,3},{2,0},{3,1},{4,6},{5,7},{6,4},{7,5},{8,10},{9,11},{10,... | collective-permute-start | bytes 786440 | tf_op jit(solution)/shard_map/ppermute | solution.py:25
  78.7 30.8 %copy-start.7 = (bf16[8,32,8,128]{3,2,1,0:T(8,128)(2,1)}, bf16[8,32,8,128]{3,2,1,0:T(8,128)(2,1)S(1)}, u32[]{:S(2)}) copy-start(bf16[8,32,8,128]{3,2,1,0:T(8,128)(2,1)S(1)} %collective-permute-done.6.refs_8_) | copy-start | bytes 1572868
  80.0 12.3 %collective-permute-start.7 = (bf16[4,32,8,128]{3,2,1,0:T(8,128)(2,1)S(1)}, bf16[4,32,8,128]{3,2,1,0:T(8,128)(2,1)S(1)}, u32[]{:S(2)}, u32[]{:S(2)}) collective-permute-start(bf16[4,32,8,128]{3,2,1,0:T(8,128)(2,1)S(1)} %add_convert_fusion.6), channel_id=1, source_target_pairs={{0,4},{4,0},{8,12},{12,8},{16,20},{20,16},{24,28},{28,24},{1,5},{5... | collective-permute-start | bytes 786440 | tf_op jit(solution)/shard_map/ppermute | solution.py:25
  82.0 29.4 %copy-start.8 = (bf16[8,32,8,128]{3,2,1,0:T(8,128)(2,1)}, bf16[8,32,8,128]{3,2,1,0:T(8,128)(2,1)S(1)}, u32[]{:S(2)}) copy-start(bf16[8,32,8,128]{3,2,1,0:T(8,128)(2,1)S(1)} %collective-permute-done.1.refs_2_) | copy-start | bytes 1572868
  82.1 12.8 %collective-permute-start.2 = (bf16[4,32,8,128]{3,2,1,0:T(8,128)(2,1)S(1)}, bf16[4,32,8,128]{3,2,1,0:T(8,128)(2,1)S(1)}, u32[]{:S(2)}, u32[]{:S(2)}) collective-permute-start(bf16[4,32,8,128]{3,2,1,0:T(8,128)(2,1)S(1)} %add_convert_fusion.7), channel_id=1, source_target_pairs={{0,2},{1,3},{2,0},{3,1},{4,6},{5,7},{6,4},{7,5},{8,10},{9,11},{10,... | collective-permute-start | bytes 786440 | tf_op jit(solution)/shard_map/ppermute | solution.py:25
  87.6 24.5 %copy-start.9 = (bf16[4,32,8,128]{3,2,1,0:T(8,128)(2,1)}, bf16[4,32,8,128]{3,2,1,0:T(8,128)(2,1)S(1)}, u32[]{:S(2)}) copy-start(bf16[4,32,8,128]{3,2,1,0:T(8,128)(2,1)S(1)} %collective-permute-done.17.refs_21_) | copy-start | bytes 786436
  88.7 6.9 %collective-permute-start.18 = (bf16[2,32,8,128]{3,2,1,0:T(8,128)(2,1)S(1)}, bf16[2,32,8,128]{3,2,1,0:T(8,128)(2,1)S(1)}, u32[]{:S(2)}, u32[]{:S(2)}) collective-permute-start(bf16[2,32,8,128]{3,2,1,0:T(8,128)(2,1)S(1)} %add_convert_fusion.8), channel_id=1, source_target_pairs={{0,8},{4,12},{8,0},{12,4},{16,24},{20,28},{24,16},{28,20},{1,9},{5... | collective-permute-start | bytes 393224 | tf_op jit(solution)/shard_map/ppermute | solution.py:25
  90.3 21.1 %copy-start.10 = (bf16[4,32,8,128]{3,2,1,0:T(8,128)(2,1)}, bf16[4,32,8,128]{3,2,1,0:T(8,128)(2,1)S(1)}, u32[]{:S(2)}) copy-start(bf16[4,32,8,128]{3,2,1,0:T(8,128)(2,1)S(1)} %collective-permute-done.12.refs_15_) | copy-start | bytes 786436
  91.4 7.8 %collective-permute-start.13 = (bf16[2,32,8,128]{3,2,1,0:T(8,128)(2,1)S(1)}, bf16[2,32,8,128]{3,2,1,0:T(8,128)(2,1)S(1)}, u32[]{:S(2)}, u32[]{:S(2)}) collective-permute-start(bf16[2,32,8,128]{3,2,1,0:T(8,128)(2,1)S(1)} %add_convert_fusion.9), channel_id=1, source_target_pairs={{0,8},{4,12},{8,0},{12,4},{16,24},{20,28},{24,16},{28,20},{1,9},{5... | collective-permute-start | bytes 393224 | tf_op jit(solution)/shard_map/ppermute | solution.py:25
  92.2 19.2 %copy-start.11 = (bf16[4,32,8,128]{3,2,1,0:T(8,128)(2,1)}, bf16[4,32,8,128]{3,2,1,0:T(8,128)(2,1)S(1)}, u32[]{:S(2)}) copy-start(bf16[4,32,8,128]{3,2,1,0:T(8,128)(2,1)S(1)} %collective-permute-done.7.refs_9_) | copy-start | bytes 786436
  93.3 9.4 %collective-permute-start.8 = (bf16[2,32,8,128]{3,2,1,0:T(8,128)(2,1)S(1)}, bf16[2,32,8,128]{3,2,1,0:T(8,128)(2,1)S(1)}, u32[]{:S(2)}, u32[]{:S(2)}) collective-permute-start(bf16[2,32,8,128]{3,2,1,0:T(8,128)(2,1)S(1)} %add_convert_fusion.10), channel_id=1, source_target_pairs={{0,8},{4,12},{8,0},{12,4},{16,24},{20,28},{24,16},{28,20},{1,9},{5... | collective-permute-start | bytes 393224 | tf_op jit(solution)/shard_map/ppermute | solution.py:25
  95.0 16.5 %copy-start.12 = (bf16[4,32,8,128]{3,2,1,0:T(8,128)(2,1)}, bf16[4,32,8,128]{3,2,1,0:T(8,128)(2,1)S(1)}, u32[]{:S(2)}) copy-start(bf16[4,32,8,128]{3,2,1,0:T(8,128)(2,1)S(1)} %collective-permute-done.2.refs_3_) | copy-start | bytes 786436
  95.0 10.0 %collective-permute-start.3 = (bf16[2,32,8,128]{3,2,1,0:T(8,128)(2,1)S(1)}, bf16[2,32,8,128]{3,2,1,0:T(8,128)(2,1)S(1)}, u32[]{:S(2)}, u32[]{:S(2)}) collective-permute-start(bf16[2,32,8,128]{3,2,1,0:T(8,128)(2,1)S(1)} %add_convert_fusion.11), channel_id=1, source_target_pairs={{0,8},{4,12},{8,0},{12,4},{16,24},{20,28},{24,16},{28,20},{1,9},{5... | collective-permute-start | bytes 393224 | tf_op jit(solution)/shard_map/ppermute | solution.py:25
  95.6 16.6 %copy-start.13 = (bf16[2,32,8,128]{3,2,1,0:T(8,128)(2,1)}, bf16[2,32,8,128]{3,2,1,0:T(8,128)(2,1)S(1)}, u32[]{:S(2)}) copy-start(bf16[2,32,8,128]{3,2,1,0:T(8,128)(2,1)S(1)} %collective-permute-done.18.refs_22_) | copy-start | bytes 393220
  96.5 10.3 %collective-permute-start.19 = (bf16[1,32,8,128]{3,2,1,0:T(8,128)(2,1)S(1)}, bf16[1,32,8,128]{3,2,1,0:T(8,128)(2,1)S(1)}, u32[]{:S(2)}, u32[]{:S(2)}) collective-permute-start(bf16[1,32,8,128]{3,2,1,0:T(8,128)(2,1)S(1)} %add_convert_fusion.12), channel_id=1, source_target_pairs={{0,16},{4,20},{8,24},{12,28},{16,0},{20,4},{24,8},{28,12},{1,17},{... | collective-permute-start | bytes 196616 | tf_op jit(solution)/shard_map/ppermute | solution.py:25
  99.2 12.3 %copy-start.14 = (bf16[2,32,8,128]{3,2,1,0:T(8,128)(2,1)}, bf16[2,32,8,128]{3,2,1,0:T(8,128)(2,1)S(1)}, u32[]{:S(2)}) copy-start(bf16[2,32,8,128]{3,2,1,0:T(8,128)(2,1)S(1)} %collective-permute-done.13.refs_16_) | copy-start | bytes 393220
  100.1 9.4 %collective-permute-start.14 = (bf16[1,32,8,128]{3,2,1,0:T(8,128)(2,1)S(1)}, bf16[1,32,8,128]{3,2,1,0:T(8,128)(2,1)S(1)}, u32[]{:S(2)}, u32[]{:S(2)}) collective-permute-start(bf16[1,32,8,128]{3,2,1,0:T(8,128)(2,1)S(1)} %add_convert_fusion.13), channel_id=1, source_target_pairs={{0,16},{4,20},{8,24},{12,28},{16,0},{20,4},{24,8},{28,12},{1,17},{... | collective-permute-start | bytes 196616 | tf_op jit(solution)/shard_map/ppermute | solution.py:25
  102.7 8.8 %copy-start.15 = (bf16[2,32,8,128]{3,2,1,0:T(8,128)(2,1)}, bf16[2,32,8,128]{3,2,1,0:T(8,128)(2,1)S(1)}, u32[]{:S(2)}) copy-start(bf16[2,32,8,128]{3,2,1,0:T(8,128)(2,1)S(1)} %collective-permute-done.8.refs_10_) | copy-start | bytes 393220
  103.7 7.8 %collective-permute-start.9 = (bf16[1,32,8,128]{3,2,1,0:T(8,128)(2,1)S(1)}, bf16[1,32,8,128]{3,2,1,0:T(8,128)(2,1)S(1)}, u32[]{:S(2)}, u32[]{:S(2)}) collective-permute-start(bf16[1,32,8,128]{3,2,1,0:T(8,128)(2,1)S(1)} %add_convert_fusion.14), channel_id=1, source_target_pairs={{0,16},{4,20},{8,24},{12,28},{16,0},{20,4},{24,8},{28,12},{1,17},{... | collective-permute-start | bytes 196616 | tf_op jit(solution)/shard_map/ppermute | solution.py:25
  105.1 6.4 %copy-start.16 = (bf16[2,32,8,128]{3,2,1,0:T(8,128)(2,1)}, bf16[2,32,8,128]{3,2,1,0:T(8,128)(2,1)S(1)}, u32[]{:S(2)}) copy-start(bf16[2,32,8,128]{3,2,1,0:T(8,128)(2,1)S(1)} %collective-permute-done.3.refs_4_) | copy-start | bytes 393220
  105.1 7.0 %collective-permute-start.4 = (bf16[1,32,8,128]{3,2,1,0:T(8,128)(2,1)S(1)}, bf16[1,32,8,128]{3,2,1,0:T(8,128)(2,1)S(1)}, u32[]{:S(2)}, u32[]{:S(2)}) collective-permute-start(bf16[1,32,8,128]{3,2,1,0:T(8,128)(2,1)S(1)} %add_convert_fusion.15), channel_id=1, source_target_pairs={{0,16},{4,20},{8,24},{12,28},{16,0},{20,4},{24,8},{28,12},{1,17},{... | collective-permute-start | bytes 196616 | tf_op jit(solution)/shard_map/ppermute | solution.py:25
  106.8 5.3 %copy-start.17 = (bf16[1,32,8,128]{3,2,1,0:T(8,128)(2,1)}, bf16[1,32,8,128]{3,2,1,0:T(8,128)(2,1)S(1)}, u32[]{:S(2)}) copy-start(bf16[1,32,8,128]{3,2,1,0:T(8,128)(2,1)S(1)} %collective-permute-done.19.refs_23_) | copy-start | bytes 196612
  109.5 2.6 %copy-start.18 = (bf16[1,32,8,128]{3,2,1,0:T(8,128)(2,1)}, bf16[1,32,8,128]{3,2,1,0:T(8,128)(2,1)S(1)}, u32[]{:S(2)}) copy-start(bf16[1,32,8,128]{3,2,1,0:T(8,128)(2,1)S(1)} %collective-permute-done.14.refs_17_) | copy-start | bytes 196612
  111.5 0.7 copy-start.19
  112.2 0.6 copy-start.20
